TPU v7x, 32 devices: a whole 2x2x4 slice. The times are simulated.
32 devices in a mesh: parts: 2 (over y), row: 4 (over z), col: 4 (over x, core).
Axes of the slice: x: 2, y: 2, z: 4, core: 2. Of those that a mesh axis runs over, the one named last changes fastest.
Arguments:
- sigma_anc: float32 [24576, 12288], P(('parts', 'row'), 'col'), parts along dimension 0
- normal_factor: float32 [4, 12288, 512], P('parts', ('col', 'row')), parts along dimension 0, may hold values from -0.078125 to 0.078125
- jj_inverse: float32 [4, 512, 512], P('parts', None, 'col'), parts along dimension 0, may hold values from -6 to 6
- blocks: int32 [4, 128], P('parts'), parts along dimension 0, may hold values from 0 to 255, as said below
Outputs:
- sigma_rj: float32 [4, 12288, 512], P('parts', 'row', 'col'), parts along dimension 0
- sigma_jj: float32 [4, 512, 512], P('parts', None, 'col'), parts along dimension 0
There are 2 independent parts, one for each index of `parts`. A program takes and returns all parts, laid end to end along the dimension named above; each array names one. Nothing has to cross between parts.
Inputs may be any that keep to these rules, and one draw needn't show every extreme that they name: Each list names 128 different blocks and always holds block 0 and block 255.
All inputs are finite; a program needn't handle non-finite values.
Results may differ from a plain program's by a relative error of at most 0.0001.
Values sent between devices are 32-bit elements; how exact they have to be, the bound alone decides.
A program may use at most 192 MiB of HBM per device.

v0:
```python
import jax
import jax.numpy as jnp
from jax import lax
from jax.sharding import PartitionSpec as P

BLK = 48


def broadcast(value, axis, source):
    kept = jnp.where(lax.axis_index(axis) == source, value, 0).astype(value.dtype)
    return lax.psum(kept, axis)


def listed_mask(blocks, first_block, count, rows):
    block_ids = first_block + jnp.arange(count, dtype=jnp.int32)
    listed = jnp.any(blocks[:, :, None] == block_ids[None, None, :], axis=1).astype(jnp.float32)
    return jnp.repeat(listed, BLK, axis=1, total_repeat_length=rows)[:, :, None]


def shards(sigma_anc, normal_factor, jj_inverse, blocks):
    tile_rows, tile_cols = sigma_anc.shape
    row_count = lax.axis_size("row")
    row_index = lax.axis_index("row")
    col_index = lax.axis_index("col")
    local_rows = normal_factor.shape[1]
    local_blocks = local_rows // BLK
    first_local = (col_index * row_count + row_index) * local_blocks
    masked = normal_factor * listed_mask(blocks, first_local, local_blocks, local_rows)
    row_blocks = tile_rows // BLK
    row_mask = listed_mask(blocks, row_index * row_blocks, row_blocks, tile_rows)
    start_row = row_index * tile_rows
    root_col = start_row // tile_cols
    offset = jnp.clip(start_row - col_index * tile_cols, 0, tile_cols - tile_rows)
    partial_list = []
    slab_list = []
    for supernode in range(2):
        gathered = lax.all_gather(masked[supernode], "row", axis=0, tiled=True)
        partial_list.append(
            jnp.dot(
                sigma_anc,
                gathered,
                precision=lax.Precision.HIGHEST,
                preferred_element_type=jnp.float32,
            )
        )
        slab_list.append(lax.dynamic_slice_in_dim(gathered, offset, tile_rows, 0))
    partials = jnp.stack(partial_list)
    slabs = jnp.stack(slab_list)
    summed = lax.psum(partials, "col")
    full_rj = -(summed * row_mask)
    part_cols = jj_inverse.shape[2]
    sigma_rj = lax.dynamic_slice_in_dim(full_rj, col_index * part_cols, part_cols, 2)
    owner_rows = broadcast(slabs, "col", root_col)
    update = jnp.einsum("srw,srv->swv", owner_rows, sigma_rj, precision=lax.Precision.HIGHEST)
    sigma_jj = jj_inverse - lax.psum(update, "row")
    return (sigma_rj, sigma_jj)


def solution(mesh):
    placed = (
        P(("parts", "row"), "col"),
        P("parts", ("col", "row"), None),
        P("parts", None, "col"),
        P("parts", None),
    )
    return jax.shard_map(
        shards,
        mesh=mesh,
        in_specs=placed,
        out_specs=(P("parts", "row", "col"), P("parts", None, "col")),
        check_vma=False,
    )
```

profile of v0, /device:TPU:19, one launch (start us, length us, event | category | flops | bytes accessed | tf_op | source)
XLA Modules:
  0.0 812.4 jit_solution(12783318977597875389)
XLA Ops:
  7.2 0.0 all-gather.5.cloned.1.call-start
  7.2 0.9 compare_reduce_fusion.1
  8.1 0.1 copy.11
  8.2 0.7 pad_clamp_fusion
  8.9 1.6 gather_fusion
  10.5 0.1 copy.12
  10.6 2.4 copy.13
  13.0 0.2 broadcast_multiply_fusion
  13.2 1.9 fusion.11
  15.1 0.0 all-gather.5.cloned.1.call-update
  15.1 0.0 all-gather.7.cloned.1.call-start
  15.2 0.7 all-gather.7.cloned.1.call-update
  15.9 0.0 all-reduce.6.cloned.1.call-start
  16.0 113.9 %all-gather.5.cloned.1.call-done = f32[1,3072,512]{1,2,0:T(8,128)} async-done(((f32[1,768,512]{1,2,0:T(8,128)}), f32[1,3072,512]{1,2,0:T(8,128)}) %all-gather.5.cloned.1.call-update) | async-done | bytes 6291472 | tf_op jit(solution)/shard_map/all_gather | solution.py:37
  129.9 67.8 %fusion.4 = f32[1,3072,512]{1,2,0:T(8,128)} fusion(f32[3072,3072]{1,0:T(8,128)} %param.8, f32[1,3072,512]{1,2,0:T(8,128)} %all-gather.5.cloned.1.call-done), kind=kOutput, calls=%fused_computation.8 | convolution fusion | flops 57982058496 | bytes 50331648 | tf_op jit(solution)/shard_map/dot_general | solution.py:39
  197.7 47.4 %all-gather.7.cloned.1.call-done = f32[1,3072,512]{1,2,0:T(8,128)} async-done(((f32[1,768,512]{1,2,0:T(8,128)}), f32[1,3072,512]{1,2,0:T(8,128)}) %all-gather.7.cloned.1.call-update) | async-done | bytes 6291472 | tf_op jit(solution)/shard_map/all_gather | solution.py:37
  245.0 0.0 copy-start
  245.0 0.0 copy-start.1
  245.0 68.0 %fusion.7 = f32[1,3072,512]{1,2,0:T(8,128)} fusion(f32[3072,3072]{1,0:T(8,128)} %param.8, f32[1,3072,512]{1,2,0:T(8,128)} %all-gather.7.cloned.1.call-done), kind=kOutput, calls=%fused_computation.9 | convolution fusion | flops 57982058496 | bytes 50331648 | tf_op jit(solution)/shard_map/dot_general | solution.py:39
  313.0 0.0 copy-done
  313.0 0.0 copy-done.1
  313.0 14.6 %pad_maximum_fusion = (f32[2,3072,512]{1,2,0:T(8,128)}, f32[2,3072,512]{1,2,0:T(8,128)}) fusion(f32[1,3072,512]{1,2,0:T(8,128)} %fusion.7, f32[1,3072,512]{1,2,0:T(8,128)} %fusion.4, f32[1,3072,512]{1,2,0:T(8,128)S(1)} %copy-done.1, f32[1,3072,512]{1,2,0:T(8,128)S(1)} %copy-done, pred[]{:T(512)S(6)} %eq.35), kind=kLoop, calls=%fused_computation.2 | loop fusion | flops 9437184 | bytes 50331648 | tf_op jit(solution)/shard_map/stack | solution.py:47
  327.6 0.0 copy-start.3
  327.6 0.0 copy-start.2
  327.6 0.0 all-reduce.6.cloned.1.call-update
  327.6 0.0 all-reduce.4.cloned.1.call-start
  327.7 0.6 copy-done.3
  328.2 0.2 compare_reduce_fusion
  328.4 0.1 copy.14
  328.5 0.0 copy-done.2
  328.5 8.1 gather_fusion.1
  336.7 0.5 copy.15
  337.1 413.7 %all-reduce.6.cloned.1.call-done = (f32[2,3072,512]{1,2,0:T(8,128)}, f32[2,3072,512]{1,2,0:T(8,128)}) async-done(((f32[2,3072,512]{1,2,0:T(8,128)}, f32[2,3072,512]{1,2,0:T(8,128)}), (f32[2,3072,512]{1,2,0:T(8,128)}, f32[2,3072,512]{1,2,0:T(8,128)})) %all-reduce.6.cloned.1.call-update) | async-done | bytes 25165840 | tf_op jit(solution)/shard_map/psum | solution.py:49
  750.9 2.2 fusion.10
  753.1 13.8 %fusion.12 = f32[2,512,128]{2,1,0:T(8,128)} fusion(f32[2,3072,512]{1,2,0:T(8,128)} %get-tuple-element.31, f32[2,3072,128]{1,2,0:T(8,128)S(1)} %fusion.10), kind=kOutput, calls=%fused_computation.20 | convolution fusion | flops 4831838208 | bytes 16252928 | tf_op jit(solution)/shard_map/srw,srv->swv/dot_general | solution.py:54
  766.9 0.0 all-reduce.4.cloned.1.call-update
  766.9 2.4 copy.17
  769.3 34.6 %all-reduce.4.cloned.1.call-done = f32[2,512,128]{2,1,0:T(8,128)} async-done(((f32[2,512,128]{2,1,0:T(8,128)}), f32[2,512,128]{2,1,0:T(8,128)}) %all-reduce.4.cloned.1.call-update) | async-done | bytes 524304 | tf_op jit(solution)/shard_map/psum | solution.py:55
  803.9 2.0 sub.7
  (5 shorter events, 0.0 us)
Async XLA Ops:
  7.2 122.7 %all-gather.5.cloned.1.call-start = ((), (), s32[]{:S(2)}) async-start(), calls=%async_computation.1 | async-start | bytes 7864320 | tf_op jit(solution)/shard_map/all_gather | solution.py:37
  15.1 229.9 %all-gather.7.cloned.1.call-start = ((), (), s32[]{:S(2)}) async-start(), calls=%async_computation.2 | async-start | bytes 7864320 | tf_op jit(solution)/shard_map/all_gather | solution.py:37
  15.9 735.0 %all-reduce.6.cloned.1.call-start = ((), (), s32[]{:S(2)}) async-start(), calls=%async_computation.3 | async-start | bytes 50331648 | tf_op jit(solution)/shard_map/psum | solution.py:49
  245.0 68.0 %copy-start = (f32[1,3072,512]{1,2,0:T(8,128)S(1)}, f32[1,3072,512]{1,2,0:T(8,128)}, u32[]{:S(2)}) copy-start(f32[1,3072,512]{1,2,0:T(8,128)} %all-gather.5.cloned.1.call-done) | copy-start | bytes 18874372
  245.0 68.0 %copy-start.1 = (f32[1,3072,512]{1,2,0:T(8,128)S(1)}, f32[1,3072,512]{1,2,0:T(8,128)}, u32[]{:S(2)}) copy-start(f32[1,3072,512]{1,2,0:T(8,128)} %all-gather.7.cloned.1.call-done) | copy-start | bytes 18874372
  327.6 0.7 copy-start.3
  327.6 1.0 copy-start.2
  327.6 476.3 %all-reduce.4.cloned.1.call-start = ((), (), s32[]{:S(2)}) async-start(), calls=%async_computation | async-start | bytes 1048576 | tf_op jit(solution)/shard_map/psum | solution.py:55
Sparse Core Ops, SparseCore 0:
  15.3 114.5 all-gather.4
  131.4 113.5 all-gather.6
  327.7 423.1 all-reduce.5
  767.1 36.7 all-reduce.3
where the time goes:
time: 817 us; the launch traced here: 812 us
  waiting for transfers between devices  610 us (75%)
  matrix products  150 us (18%)
  other arithmetic  20.8 us (3%)
  local copies, waits for them, and re-layouts  17.7 us (2%)
  between operations  13.9 us (2%)
    psum x1, waiting for transfers between devices, shards(): summed = lax.psum(partials, 'col')  414 us
    all_gather x2, waiting for transfers between devices, shards(): gathered = lax.all_gather(masked[supernode], 'row', axis=0, tiled=True)  161 us
    dot_general x2, matrix products, shards(): jnp.dot(sigma_anc, gathered, precision=lax.Precision.HIGHEST, preferred_e...  136 us
    psum x1, waiting for transfers between devices, shards(): sigma_jj = jj_inverse - lax.psum(update, 'row')  34.6 us
  transfers between devices with their start and end apart: 4, of which 4 were waited for; matrix products, arithmetic and copies ran while one was open for 10% of the time, Pallas kernels for 0%

commit v1 on v0

--- a/solution.py
+++ b/solution.py
@@ -4,11 +4,6 @@
 from jax.sharding import PartitionSpec as P
 
 BLK = 48
-
-
-def broadcast(value, axis, source):
-    kept = jnp.where(lax.axis_index(axis) == source, value, 0).astype(value.dtype)
-    return lax.psum(kept, axis)
 
 
 def listed_mask(blocks, first_block, count, rows):
@@ -31,29 +26,30 @@
     start_row = row_index * tile_rows
     root_col = start_row // tile_cols
     offset = jnp.clip(start_row - col_index * tile_cols, 0, tile_cols - tile_rows)
-    partial_list = []
-    slab_list = []
+    is_root = (col_index == root_col).astype(jnp.float32)
+    rj_list = []
+    update_list = []
     for supernode in range(2):
         gathered = lax.all_gather(masked[supernode], "row", axis=0, tiled=True)
-        partial_list.append(
-            jnp.dot(
-                sigma_anc,
-                gathered,
-                precision=lax.Precision.HIGHEST,
-                preferred_element_type=jnp.float32,
-            )
+        partial = jnp.dot(
+            sigma_anc,
+            gathered,
+            precision=lax.Precision.HIGH,
+            preferred_element_type=jnp.float32,
         )
-        slab_list.append(lax.dynamic_slice_in_dim(gathered, offset, tile_rows, 0))
-    partials = jnp.stack(partial_list)
-    slabs = jnp.stack(slab_list)
-    summed = lax.psum(partials, "col")
-    full_rj = -(summed * row_mask)
-    part_cols = jj_inverse.shape[2]
-    sigma_rj = lax.dynamic_slice_in_dim(full_rj, col_index * part_cols, part_cols, 2)
-    owner_rows = broadcast(slabs, "col", root_col)
-    update = jnp.einsum("srw,srv->swv", owner_rows, sigma_rj, precision=lax.Precision.HIGHEST)
-    sigma_jj = jj_inverse - lax.psum(update, "row")
-    return (sigma_rj, sigma_jj)
+        own_rj = -lax.psum_scatter(partial * row_mask[supernode], "col", scatter_dimension=1, tiled=True)
+        rj_list.append(own_rj)
+        wide_rj = lax.all_gather(own_rj, "col", axis=1, tiled=True)
+        slab = lax.dynamic_slice_in_dim(gathered, offset, tile_rows, 0) * is_root
+        update = lax.dot_general(
+            slab,
+            wide_rj,
+            (((0,), (0,)), ((), ())),
+            precision=lax.Precision.HIGH,
+            preferred_element_type=jnp.float32,
+        )
+        update_list.append(lax.psum(lax.psum_scatter(update, "col", scatter_dimension=1, tiled=True), "row"))
+    return (jnp.stack(rj_list), jj_inverse - jnp.stack(update_list))
 
 
 def solution(mesh):

time: 817 us -> 576 us (0.71)
  waiting for transfers between devices: 610 us -> 362 us
  matrix products: 150 us -> 162 us
    psum x2 -> x1, waiting for transfers between devices: 448 us -> 35.4 us  [shards(): lax.psum(lax.psum_scatter(update, 'col', scatter_dimension=1, tiled=True)...]
    reduce_scatter x0 -> x4, waiting for transfers between devices: none -> 94.6 us  [the longest x2 54.1 us: shards(): lax.psum_scatter(partial * row_mask[supernode], 'col', scatter_dimension=...]
    all_gather x0 -> x2, waiting for transfers between devices: none -> 78.4 us  [shards(): wide_rj = lax.all_gather(own_rj, 'col', axis=1, tiled=True)]
    another operation x1, other arithmetic: 14.6 us -> 2.09 us  [shards(): return (jnp.stack(rj_list), jj_inverse - jnp.stack(update_list))]
    dot_general x3 -> x4, matrix products: 150 us -> 162 us  [the longest x2 133 us: shards(): jnp.dot(sigma_anc, gathered, precision=lax.Precision.HIGH, preferred_elem...]
  transfers between devices with their start and end apart: 4 -> 9, of which waited for: 4 -> 8; matrix products, arithmetic and copies ran while one was open for 10% -> 32% of each run, Pallas kernels for 0% -> 0%
where the time goes in v1:
time: 576 us; the launch traced here: 570 us
  waiting for transfers between devices  362 us (63%)
  matrix products  162 us (28%)
  local copies, waits for them, and re-layouts  15.7 us (3%)
  other arithmetic  14.9 us (3%)
  between operations  14.2 us (2%)
    all_gather x2, waiting for transfers between devices, shards(): gathered = lax.all_gather(masked[supernode], 'row', axis=0, tiled=True)  153 us
    dot_general x2, matrix products, shards(): jnp.dot(sigma_anc, gathered, precision=lax.Precision.HIGH, preferred_elem...  133 us
    all_gather x2, waiting for transfers between devices, shards(): wide_rj = lax.all_gather(own_rj, 'col', axis=1, tiled=True)  78.4 us
    reduce_scatter x2, waiting for transfers between devices, shards(): lax.psum_scatter(partial * row_mask[supernode], 'col', scatter_dimension=...  54.1 us
    reduce_scatter x2, waiting for transfers between devices, shards(): lax.psum_scatter(update, 'col', scatter_dimension=1, tiled=True)  40.5 us
    psum x1, waiting for transfers between devices, shards(): lax.psum(lax.psum_scatter(update, 'col', scatter_dimension=1, tiled=True)...  35.4 us
    dot_general x2, matrix products, shards(): lax.dot_general(slab, wide_rj, (((0,), (0,)), ((), ())), precision=lax.Pr...  29.3 us
  transfers between devices with their start and end apart: 9, of which 8 were waited for; matrix products, arithmetic and copies ran while one was open for 32% of the time, Pallas kernels for 0%

profile of v1, /device:TPU:19, one launch (start us, length us, event | category | flops | bytes accessed | tf_op | source)
XLA Modules:
  0.0 569.6 jit_solution(10979280178893593499)
XLA Ops:
  7.2 0.0 all-gather.11.cloned.1.call-start
  7.2 0.9 compare_reduce_fusion.1
  8.1 0.1 copy.10
  8.2 0.7 pad_clamp_fusion
  8.9 1.6 gather_fusion
  10.5 0.1 copy.11
  10.6 2.2 broadcast_multiply_fusion
  12.8 0.0 copy-start
  12.8 2.0 fusion.12
  14.8 0.0 all-gather.11.cloned.1.call-update
  14.8 0.0 all-gather.13.cloned.1.call-start
  14.9 0.7 all-gather.13.cloned.1.call-update
  15.6 0.0 reduce-scatter.5.cloned.1.call-start
  15.6 0.2 compare_reduce_fusion
  15.8 0.1 copy.12
  15.9 8.1 %gather_fusion.1 = f32[3072,2]{1,0:T(8,128)S(1)} fusion(f32[2,64]{0,1:T(8,128)S(1)} %copy.12, s32[3072]{0:T(1024)S(1)} %broadcast_clamp_fusion), kind=kCustom, calls=%fused_computation.1 | custom fusion | bytes 61440 | tf_op jit(solution)/shard_map/jit(_take)/gather | solution.py:12
  24.1 1.3 slice_reduce_fusion.1
  25.4 104.2 %all-gather.11.cloned.1.call-done = f32[1,3072,512]{2,1,0:T(8,128)} async-done(((f32[1,768,512]{2,1,0:T(8,128)}), f32[1,3072,512]{2,1,0:T(8,128)}) %all-gather.11.cloned.1.call-update) | async-done | bytes 6291472 | tf_op jit(solution)/shard_map/all_gather | solution.py:33
  129.6 66.1 %multiply_bitcast_fusion.1 = f32[3072,512]{0,1:T(8,128)} fusion(f32[3072,3072]{1,0:T(8,128)} %param.8, f32[1,3072,512]{2,1,0:T(8,128)} %all-gather.11.cloned.1.call-done, f32[3072]{0:T(1024)S(1)} %get-tuple-element.32), kind=kOutput, calls=%fused_computation.11 | convolution fusion | flops 28992602112 | bytes 50343936 | tf_op jit(solution)/shard_map/dot_general | solution.py:34
  195.7 0.0 reduce-scatter.5.cloned.1.call-update
  195.7 0.0 reduce-scatter.7.cloned.1.call-start
  195.8 49.0 %all-gather.13.cloned.1.call-done = f32[1,3072,512]{2,1,0:T(8,128)} async-done(((f32[1,768,512]{2,1,0:T(8,128)}), f32[1,3072,512]{2,1,0:T(8,128)}) %all-gather.13.cloned.1.call-update) | async-done | bytes 6291472 | tf_op jit(solution)/shard_map/all_gather | solution.py:33
  244.7 66.6 %multiply_bitcast_fusion = f32[3072,512]{0,1:T(8,128)} fusion(f32[3072,3072]{1,0:T(8,128)} %param.8, f32[1,3072,512]{2,1,0:T(8,128)} %all-gather.13.cloned.1.call-done, f32[3072]{0:T(1024)S(1)} %get-tuple-element.33), kind=kOutput, calls=%fused_computation.10 | convolution fusion | flops 28992602112 | bytes 50343936 | tf_op jit(solution)/shard_map/dot_general | solution.py:34
  311.4 0.0 reduce-scatter.7.cloned.1.call-update
  311.4 0.0 all-gather.7.cloned.1.call-start
  311.4 0.0 reduce-scatter.5.cloned.1.call-done
  311.5 3.4 fusion.13
  314.9 0.0 all-gather.7.cloned.1.call-update
  314.9 0.0 all-gather.9.cloned.1.call-start
  315.0 54.0 %reduce-scatter.7.cloned.1.call-done = f32[3072,128]{0,1:T(8,128)} async-done(((f32[3072,512]{0,1:T(8,128)}), f32[3072,128]{0,1:T(8,128)}) %reduce-scatter.7.cloned.1.call-update) | async-done | bytes 1572880 | tf_op jit(solution)/shard_map/reduce_scatter | solution.py:40
  369.0 3.4 fusion.14
  372.4 0.0 all-gather.9.cloned.1.call-update
  372.5 0.0 reduce-scatter.9.cloned.1.call-start
  372.5 44.7 %all-gather.7.cloned.1.call-done = f32[3072,512]{0,1:T(8,128)} async-done(((f32[3072,128]{0,1:T(8,128)}), f32[3072,512]{0,1:T(8,128)}) %all-gather.7.cloned.1.call-update) | async-done | bytes 6291472 | tf_op jit(solution)/shard_map/all_gather | solution.py:42
  417.3 14.7 %fusion.5 = f32[512,512]{1,0:T(8,128)} fusion(f32[3072,512]{0,1:T(8,128)} %all-gather.7.cloned.1.call-done, f32[1,3072,512]{2,1,0:T(8,128)} %all-gather.11.cloned.1.call-done, f32[]{:T(128)S(6)} %convert_element_type.11), kind=kOutput, calls=%fused_computation.9 | convolution fusion | flops 4833411072 | bytes 13631492 | tf_op jit(solution)/shard_map/dot_general | solution.py:44
  431.9 0.0 reduce-scatter.9.cloned.1.call-update
  432.0 0.0 reduce-scatter.11.cloned.1.call-start
  432.0 33.7 %all-gather.9.cloned.1.call-done = f32[3072,512]{0,1:T(8,128)} async-done(((f32[3072,128]{0,1:T(8,128)}), f32[3072,512]{0,1:T(8,128)}) %all-gather.9.cloned.1.call-update) | async-done | bytes 6291472 | tf_op jit(solution)/shard_map/all_gather | solution.py:42
  465.7 14.6 %fusion.2 = f32[512,512]{1,0:T(8,128)} fusion(f32[3072,512]{0,1:T(8,128)} %all-gather.9.cloned.1.call-done, f32[1,3072,512]{2,1,0:T(8,128)} %all-gather.13.cloned.1.call-done, f32[]{:T(128)S(6)} %convert_element_type.11), kind=kOutput, calls=%fused_computation.5 | convolution fusion | flops 4833411072 | bytes 13631492 | tf_op jit(solution)/shard_map/dot_general | solution.py:44
  480.3 0.0 reduce-scatter.11.cloned.1.call-update
  480.3 0.0 all-reduce.3.cloned.1.call-start
  480.4 12.3 %reduce-scatter.9.cloned.1.call-done = f32[512,128]{1,0:T(8,128)} async-done(((f32[512,512]{1,0:T(8,128)}), f32[512,128]{1,0:T(8,128)}) %reduce-scatter.9.cloned.1.call-update) | async-done | bytes 262160 | tf_op jit(solution)/shard_map/reduce_scatter | solution.py:51
  492.7 28.2 %reduce-scatter.11.cloned.1.call-done = f32[512,128]{1,0:T(8,128)} async-done(((f32[512,512]{1,0:T(8,128)}), f32[512,128]{1,0:T(8,128)}) %reduce-scatter.11.cloned.1.call-update) | async-done | bytes 262160 | tf_op jit(solution)/shard_map/reduce_scatter | solution.py:51
  520.9 0.0 all-reduce.3.cloned.1.call-update
  521.0 2.1 pad_maximum_fusion
  523.1 2.4 copy.13
  525.4 35.4 %all-reduce.3.cloned.1.call-done = (f32[1,512,128]{2,1,0:T(8,128)}, f32[1,512,128]{2,1,0:T(8,128)}) async-done(((f32[1,512,128]{2,1,0:T(8,128)}, f32[1,512,128]{2,1,0:T(8,128)}), (f32[1,512,128]{2,1,0:T(8,128)}, f32[1,512,128]{2,1,0:T(8,128)})) %all-reduce.3.cloned.1.call-update) | async-done | bytes 524304 | tf_op jit(solution)/shard_map/psum | solution.py:51
  560.9 2.0 maximum_subtract_fusion
  (8 shorter events, 0.0 us)
Async XLA Ops:
  7.2 122.4 %all-gather.11.cloned.1.call-start = ((), (), s32[]{:S(2)}) async-start(), calls=%async_computation.10 | async-start | bytes 7864320 | tf_op jit(solution)/shard_map/all_gather | solution.py:33
  12.8 2.8 copy-start.1
  12.8 3.1 copy-start
  14.8 229.9 %all-gather.13.cloned.1.call-start = ((), (), s32[]{:S(2)}) async-start(), calls=%async_computation.11 | async-start | bytes 7864320 | tf_op jit(solution)/shard_map/all_gather | solution.py:33
  15.6 295.9 %reduce-scatter.5.cloned.1.call-start = ((), (), s32[]{:S(2)}) async-start(), calls=%async_computation.4 | async-start | bytes 7864320 | tf_op jit(solution)/shard_map/reduce_scatter | solution.py:40
  195.7 173.3 %reduce-scatter.7.cloned.1.call-start = ((), (), s32[]{:S(2)}) async-start(), calls=%async_computation.5 | async-start | bytes 7864320 | tf_op jit(solution)/shard_map/reduce_scatter | solution.py:40
  311.4 105.9 %all-gather.7.cloned.1.call-start = ((), (), s32[]{:S(2)}) async-start(), calls=%async_computation.6 | async-start | bytes 7864320 | tf_op jit(solution)/shard_map/all_gather | solution.py:42
  314.9 150.7 %all-gather.9.cloned.1.call-start = ((), (), s32[]{:S(2)}) async-start(), calls=%async_computation.8 | async-start | bytes 7864320 | tf_op jit(solution)/shard_map/all_gather | solution.py:42
  372.5 120.3 %reduce-scatter.9.cloned.1.call-start = ((), (), s32[]{:S(2)}) async-start(), calls=%async_computation.7 | async-start | bytes 1310720 | tf_op jit(solution)/shard_map/reduce_scatter | solution.py:51
  432.0 89.0 %reduce-scatter.11.cloned.1.call-start = ((), (), s32[]{:S(2)}) async-start(), calls=%async_computation.9 | async-start | bytes 1310720 | tf_op jit(solution)/shard_map/reduce_scatter | solution.py:51
  480.3 80.5 %all-reduce.3.cloned.1.call-start = ((), (), s32[]{:S(2)}) async-start(), calls=%async_computation.12 | async-start | bytes 1048576 | tf_op jit(solution)/shard_map/psum | solution.py:51
Sparse Core Ops, SparseCore 0:
  14.9 114.5 all-gather.10
  131.1 113.5 all-gather.12
  247.3 57.4 reduce-scatter.4
  311.5 57.4 reduce-scatter.6
  370.4 46.7 all-gather.6
  419.3 46.3 all-gather.8
  468.2 24.4 reduce-scatter.8
  496.0 24.8 reduce-scatter.10
  523.3 37.4 all-reduce.2

commit v2 on v1

v2 whole, which is shorter than its diff:
```python
import functools

import jax
import jax.numpy as jnp
from jax import lax
from jax.experimental import pallas as pl
from jax.experimental.pallas import tpu as pltpu
from jax.sharding import PartitionSpec as P

BLK = 48
HALVES = 2
MESH = pl.DeviceIdType.MESH


def listed_mask(blocks, first_block, count, rows):
    block_ids = first_block + jnp.arange(count, dtype=jnp.int32)
    listed = jnp.any(blocks[:, :, None] == block_ids[None, None, :], axis=1).astype(jnp.float32)
    return jnp.repeat(listed, BLK, axis=1, total_repeat_length=rows)


def split(value):
    high = lax.reduce_precision(value, 8, 7)
    return high.astype(jnp.bfloat16), (value - high).astype(jnp.bfloat16)


def dot3(left, right, dims):
    (lh, ll), (rh, rl) = left, right

    def dot(a, b):
        return lax.dot_general(a, b, (dims, ((), ())), preferred_element_type=jnp.float32)

    return dot(lh, rh) + dot(lh, rl) + dot(ll, rh)


def diagonal_kernel(n, u_ref, jj_ref, out_ref, held, send1, recv1, send2, recv2):
    row, col = lax.axis_index("row"), lax.axis_index("col")
    me = row * n + col
    count = n * n
    piece = u_ref.shape[1] // n
    width = u_ref.shape[2] // n
    barrier = pltpu.get_barrier_semaphore()
    for step in range(1, count):
        other = lax.rem(me + step, count)
        pl.semaphore_signal(barrier, inc=1, device_id={"row": other // n, "col": lax.rem(other, n)}, device_id_type=MESH)
    pl.semaphore_wait(barrier, count - 1)

    def part_of(to_row, to_col):
        return u_ref.at[:, pl.ds(pl.multiple_of(to_row * piece, piece), piece), pl.ds(pl.multiple_of(to_col * width, width), width)]

    def scatter(step):
        other = lax.rem(me + step, count)
        to_row, to_col = other // n, lax.rem(other, n)
        return pltpu.make_async_remote_copy(
            src_ref=part_of(to_row, to_col),
            dst_ref=held.at[row],
            send_sem=send1.at[step],
            recv_sem=recv1.at[row],
            device_id={"row": to_row, "col": to_col},
            device_id_type=MESH,
        )

    @pl.when(row == col)
    def _():
        for step in range(1, count):
            scatter(step).start()
        held[row] = part_of(row, col)[...]

    for root in range(n):
        @pl.when(jnp.logical_or(row != root, col != root))
        def _():
            pltpu.make_async_remote_copy(
                src_ref=held.at[root],
                dst_ref=held.at[root],
                send_sem=send1.at[0],
                recv_sem=recv1.at[root],
                device_id={"row": lax.rem(row + 1, n)},
                device_id_type=MESH,
            ).wait_recv()

    mine = pl.ds(pl.multiple_of(row * piece, piece), piece)
    total = held[0]
    for root in range(1, n):
        total = total + held[root]
    out_ref[:, mine, :] = jj_ref[:, mine, :] - total

    def share(step):
        return pltpu.make_async_remote_copy(
            src_ref=out_ref.at[:, mine, :],
            dst_ref=out_ref.at[:, mine, :],
            send_sem=send2.at[step],
            recv_sem=recv2.at[step],
            device_id={"row": lax.rem(row + step, n)},
            device_id_type=MESH,
        )

    for step in range(1, n):
        share(step).start()
    for step in range(1, n):
        share(step).wait()

    @pl.when(row == col)
    def _():
        for step in range(1, count):
            scatter(step).wait_send()


def finish_diagonal(update, jj_inverse, n):
    supernodes, w, part_cols = jj_inverse.shape
    return pl.pallas_call(
        functools.partial(diagonal_kernel, n),
        out_shape=jax.ShapeDtypeStruct(jj_inverse.shape, jnp.float32),
        in_specs=[pl.BlockSpec(memory_space=pltpu.VMEM)] * 2,
        out_specs=pl.BlockSpec(memory_space=pltpu.VMEM),
        scratch_shapes=[
            pltpu.VMEM((n, supernodes, w // n, part_cols), jnp.float32),
            pltpu.SemaphoreType.DMA((n * n,)),
            pltpu.SemaphoreType.DMA((n,)),
            pltpu.SemaphoreType.DMA((n,)),
            pltpu.SemaphoreType.DMA((n,)),
        ],
        compiler_params=pltpu.CompilerParams(collective_id=0, has_side_effects=True),
    )(update, jj_inverse)


def shards(sigma_anc, normal_factor, jj_inverse, blocks):
    tile_rows, tile_cols = sigma_anc.shape
    row_count = lax.axis_size("row")
    col_count = lax.axis_size("col")
    row_index = lax.axis_index("row")
    col_index = lax.axis_index("col")
    supernodes, local_rows, w = normal_factor.shape
    part_cols = jj_inverse.shape[2]
    sub = part_cols // HALVES
    chunk = sub * col_count
    local_blocks = local_rows // BLK
    first_local = (col_index * row_count + row_index) * local_blocks
    masked = normal_factor * listed_mask(blocks, first_local, local_blocks, local_rows)[:, :, None]
    chunks = masked.reshape(supernodes, local_rows, col_count, HALVES, sub).transpose(0, 3, 1, 2, 4)
    chunks = chunks.reshape(supernodes, HALVES, local_rows, chunk)
    row_blocks = tile_rows // BLK
    row_mask = listed_mask(blocks, row_index * row_blocks, row_blocks, tile_rows)
    start_row = row_index * tile_rows
    root_col = start_row // tile_cols
    square = tile_rows == tile_cols
    offset = jnp.clip(start_row - col_index * tile_cols, 0, tile_cols - tile_rows)
    ah, al = split(sigma_anc)
    a3 = jnp.concatenate([ah, ah, al], axis=1)

    def slab_of(value):
        return value if square else lax.dynamic_slice_in_dim(value, offset, tile_rows, 0)

    rj_list = []
    update_list = []
    for supernode in range(supernodes):
        own_list = []
        wide_list = []
        gathered_list = []
        for half in range(HALVES):
            gathered = lax.all_gather(chunks[supernode, half], "row", axis=0, tiled=True)
            bh, bl = split(gathered)
            gathered_list.append((slab_of(bh), slab_of(bl)))
            b3 = jnp.concatenate([bh, bl, bh], axis=0)
            partial = lax.dot_general(b3, a3, (((0,), (1,)), ((), ())), preferred_element_type=jnp.float32)
            own = -lax.psum_scatter(partial * row_mask[supernode][None, :], "col", scatter_dimension=0, tiled=True)
            own_list.append(own)
            wide_list.append(split(lax.all_gather(own, "col", axis=0, tiled=True)))
        rj_list.append(jnp.concatenate(own_list, axis=0).T)
        slab = tuple(jnp.concatenate([g[i] for g in gathered_list], axis=1) for i in range(2))
        update = jnp.stack([dot3(slab, wide, ((0,), (1,))) for wide in wide_list], axis=1)
        update = update.reshape(HALVES, col_count, sub, HALVES, col_count, sub).transpose(1, 0, 2, 4, 3, 5)
        update_list.append(update.reshape(w, w))
    update = jnp.stack(update_list)
    if square and row_count == col_count:
        sigma_jj = finish_diagonal(update, jj_inverse, col_count)
    else:
        update = jnp.where(col_index == root_col, update, 0.0)
        update = lax.psum_scatter(update, "col", scatter_dimension=2, tiled=True)
        sigma_jj = jj_inverse - lax.psum(update, "row")
    return (jnp.stack(rj_list), sigma_jj)


def solution(mesh):
    placed = (
        P(("parts", "row"), "col"),
        P("parts", ("col", "row"), None),
        P("parts", None, "col"),
        P("parts", None),
    )
    return jax.shard_map(
        shards,
        mesh=mesh,
        in_specs=placed,
        out_specs=(P("parts", "row", "col"), P("parts", None, "col")),
        check_vma=False,
    )
```

time: 576 us -> 632 us (1.097)
  waiting for transfers between devices: 362 us -> 301 us
  Pallas kernels: 0 us -> 45.7 us
  other arithmetic: 14.9 us -> 57.6 us
  local copies, waits for them, and re-layouts: 15.7 us -> 52.1 us
  matrix products: 162 us -> 152 us
    all_gather x4 -> x8, waiting for transfers between devices: 232 us -> 180 us  [the longest x4 108 us: shards(): lax.all_gather(chunks[supernode, half], 'row', axis=0, tiled=True)]
    pallas_call x0 -> x1, Pallas kernels: none -> 45.7 us  [finish_diagonal(): pl.pallas_call(functools.partial(diagonal_kernel, n), out_shape=jax.Shape...]
    convert_element_type x0 -> x5, other arithmetic: none -> 35.5 us  [split(): return (high.astype(jnp.bfloat16), (value - high).astype(jnp.bfloat16))]
    psum x1 -> x0, waiting for transfers between devices: 35.4 us -> none  [shards(): lax.psum(lax.psum_scatter(update, 'col', scatter_dimension=1, tiled=True)...]
    reduce_scatter x4, waiting for transfers between devices: 94.6 us -> 119 us  [shards(): lax.psum_scatter(partial * row_mask[supernode][None, :], 'col', scatter_d...]
    another operation x0 -> x10, local copies, waits for them, and re-layouts: none -> 21.4 us  [the longest x8 15.3 us: shards(): jnp.stack([dot3(slab, wide, ((0,), (1,))) for wide in wide_list], axis=1)]
    unnamed x5 -> x69, local copies, waits for them, and re-layouts: 2.37 us -> 17.4 us
    dot_general x4 -> x16, matrix products: 162 us -> 152 us  [the longest x4 127 us: shards(): lax.dot_general(b3, a3, (((0,), (1,)), ((), ())), preferred_element_type=...]
  transfers between devices with their start and end apart: 9 -> 12, of which waited for: 8 -> 12; matrix products, arithmetic and copies ran while one was open for 32% -> 36% of each run, Pallas kernels for 0% -> 0%
where the time goes in v2:
time: 632 us; the launch traced here: 624 us
  waiting for transfers between devices  301 us (48%)
  matrix products  152 us (24%)
  other arithmetic  57.6 us (9%)
  local copies, waits for them, and re-layouts  52.1 us (8%)
  Pallas kernels  45.7 us (7%)
  between operations  14.9 us (2%)
    dot_general x4, matrix products, shards(): lax.dot_general(b3, a3, (((0,), (1,)), ((), ())), preferred_element_type=...  127 us
    reduce_scatter x4, waiting for transfers between devices, shards(): lax.psum_scatter(partial * row_mask[supernode][None, :], 'col', scatter_d...  119 us
    all_gather x4, waiting for transfers between devices, shards(): lax.all_gather(chunks[supernode, half], 'row', axis=0, tiled=True)  108 us
    all_gather x4, waiting for transfers between devices, shards(): wide_list.append(split(lax.all_gather(own, 'col', axis=0, tiled=True)))  71.3 us
    pallas_call x1, Pallas kernels, finish_diagonal(): pl.pallas_call(functools.partial(diagonal_kernel, n), out_shape=jax.Shape...  45.7 us
    convert_element_type x5, other arithmetic, split(): return (high.astype(jnp.bfloat16), (value - high).astype(jnp.bfloat16))  35.5 us
    dot_general x12, matrix products, dot(): lax.dot_general(a, b, (dims, ((), ())), preferred_element_type=jnp.float32)  25.3 us
    unnamed x69, local copies, waits for them, and re-layouts  17.4 us
  transfers between devices with their start and end apart: 12, of which 12 were waited for; matrix products, arithmetic and copies ran while one was open for 36% of the time, Pallas kernels for 0%

profile of v2, /device:TPU:19, one launch (start us, length us, event | category | flops | bytes accessed | tf_op | source)
XLA Modules:
  0.0 624.2 jit_solution(15677673720056458959)
XLA Ops:
  8.9 1.6 gather_fusion
  10.6 2.4 copy.22
  13.5 1.7 fusion.85
  17.4 25.7 %reduce-precision_convert_fusion = (bf16[3072,3072]{1,0:T(8,128)(2,1)}, bf16[3072,3072]{1,0:T(8,128)(2,1)}) fusion(f32[3072,3072]{1,0:T(8,128)} %param.8), kind=kLoop, calls=%fused_computation.4 | loop fusion | flops 37748736 | bytes 75497472 | tf_op jit(solution)/shard_map/convert_element_type | solution.py:23
  43.4 8.1 %gather_fusion.1 = f32[3072,2]{1,0:T(8,128)S(1)} fusion(f32[2,64]{0,1:T(8,128)S(1)} %copy.24, s32[3072]{0:T(1024)S(1)} %broadcast_clamp_fusion), kind=kCustom, calls=%fused_computation.1 | custom fusion | bytes 61440 | tf_op jit(solution)/shard_map/jit(_take)/gather | solution.py:18
  51.6 1.3 slice_reduce_fusion.1
  52.9 25.7 %all-gather.21.cloned.1.call-done = f32[1,1,3072,256]{2,3,1,0:T(8,128)} async-done(((f32[1,1,768,256]{2,3,1,0:T(8,128)}), f32[1,1,3072,256]{2,3,1,0:T(8,128)}) %all-gather.21.cloned.1.call-update) | async-done | bytes 3145744 | tf_op jit(solution)/shard_map/all_gather | solution.py:159
  78.6 2.5 fusion.37
  82.8 31.8 %fusion.34 = f32[256,3072]{1,0:T(8,128)} fusion(f32[3072]{0:T(1024)S(1)} %get-tuple-element.32, bf16[3072,3072]{1,0:T(8,128)(2,1)} %get-tuple-element.35, bf16[3072,3072]{1,0:T(8,128)(2,1)} %get-tuple-element.34, bf16[9216,256]{0,1:T(8,128)(2,1)S(1)} %fusion.95), kind=kOutput, calls=%fused_computation.49 | convolution fusion | flops 14666170368 | bytes 45625344 | tf_op jit(solution)/shard_map/dot_general | solution.py:163
  114.7 27.7 %all-gather.23.cloned.1.call-done = f32[1,1,3072,256]{2,3,1,0:T(8,128)} async-done(((f32[1,1,768,256]{2,3,1,0:T(8,128)}), f32[1,1,3072,256]{2,3,1,0:T(8,128)}) %all-gather.23.cloned.1.call-update) | async-done | bytes 3145744 | tf_op jit(solution)/shard_map/all_gather | solution.py:159
  142.3 2.5 fusion.38
  146.8 31.8 %fusion.31 = f32[256,3072]{1,0:T(8,128)} fusion(f32[3072]{0:T(1024)S(1)} %get-tuple-element.32, bf16[3072,3072]{1,0:T(8,128)(2,1)} %get-tuple-element.35, bf16[3072,3072]{1,0:T(8,128)(2,1)} %get-tuple-element.34, bf16[9216,256]{0,1:T(8,128)(2,1)S(1)} %fusion.93), kind=kOutput, calls=%fused_computation.48 | convolution fusion | flops 14666170368 | bytes 45625344 | tf_op jit(solution)/shard_map/dot_general | solution.py:163
  178.8 27.2 %all-gather.25.cloned.1.call-done = f32[1,1,3072,256]{2,3,1,0:T(8,128)} async-done(((f32[1,1,768,256]{2,3,1,0:T(8,128)}), f32[1,1,3072,256]{2,3,1,0:T(8,128)}) %all-gather.25.cloned.1.call-update) | async-done | bytes 3145744 | tf_op jit(solution)/shard_map/all_gather | solution.py:159
  206.1 2.5 fusion.39
  210.2 31.8 %fusion.28 = f32[256,3072]{1,0:T(8,128)} fusion(f32[3072]{0:T(1024)S(1)} %get-tuple-element.33, bf16[3072,3072]{1,0:T(8,128)(2,1)} %get-tuple-element.35, bf16[3072,3072]{1,0:T(8,128)(2,1)} %get-tuple-element.34, bf16[9216,256]{0,1:T(8,128)(2,1)S(1)} %fusion.91), kind=kOutput, calls=%fused_computation.47 | convolution fusion | flops 14666170368 | bytes 45625344 | tf_op jit(solution)/shard_map/dot_general | solution.py:163
  242.1 27.6 %all-gather.27.cloned.1.call-done = f32[1,1,3072,256]{2,3,1,0:T(8,128)} async-done(((f32[1,1,768,256]{2,3,1,0:T(8,128)}), f32[1,1,3072,256]{2,3,1,0:T(8,128)}) %all-gather.27.cloned.1.call-update) | async-done | bytes 3145744 | tf_op jit(solution)/shard_map/all_gather | solution.py:159
  269.7 2.5 fusion.40
  274.1 31.7 %fusion.25 = f32[256,3072]{1,0:T(8,128)} fusion(f32[3072]{0:T(1024)S(1)} %get-tuple-element.33, bf16[3072,3072]{1,0:T(8,128)(2,1)} %get-tuple-element.35, bf16[3072,3072]{1,0:T(8,128)(2,1)} %get-tuple-element.34, bf16[9216,256]{0,1:T(8,128)(2,1)S(1)} %fusion.89), kind=kOutput, calls=%fused_computation.46 | convolution fusion | flops 14666170368 | bytes 45625344 | tf_op jit(solution)/shard_map/dot_general | solution.py:163
  305.9 3.2 reduce-scatter.5.cloned.1.call-done
  309.1 2.1 neg.12
  311.3 38.4 %reduce-scatter.7.cloned.1.call-done = f32[64,3072]{1,0:T(8,128)} async-done(((f32[256,3072]{1,0:T(8,128)}), f32[64,3072]{1,0:T(8,128)}) %reduce-scatter.7.cloned.1.call-update) | async-done | bytes 786448 | tf_op jit(solution)/shard_map/reduce_scatter | solution.py:164
  349.7 2.1 neg.13
  351.9 38.4 %reduce-scatter.9.cloned.1.call-done = f32[64,3072]{1,0:T(8,128)} async-done(((f32[256,3072]{1,0:T(8,128)}), f32[64,3072]{1,0:T(8,128)}) %reduce-scatter.9.cloned.1.call-update) | async-done | bytes 786448 | tf_op jit(solution)/shard_map/reduce_scatter | solution.py:164
  390.2 2.1 neg.14
  392.4 39.1 %reduce-scatter.11.cloned.1.call-done = f32[64,3072]{1,0:T(8,128)} async-done(((f32[256,3072]{1,0:T(8,128)}), f32[64,3072]{1,0:T(8,128)}) %reduce-scatter.11.cloned.1.call-update) | async-done | bytes 786448 | tf_op jit(solution)/shard_map/reduce_scatter | solution.py:164
  431.5 2.1 neg.15
  436.6 2.7 copy.29
  439.3 22.7 %all-gather.13.cloned.1.call-done = f32[256,3072]{1,0:T(8,128)} async-done(((f32[64,3072]{1,0:T(8,128)}), f32[256,3072]{1,0:T(8,128)}) %all-gather.13.cloned.1.call-update) | async-done | bytes 3145744 | tf_op jit(solution)/shard_map/all_gather | solution.py:166
  462.0 4.0 fusion.73
  468.1 1.9 fusion.57
  470.0 2.5 stack.33
  472.5 3.6 copy.25
  476.1 15.9 %all-gather.15.cloned.1.call-done = f32[256,3072]{1,0:T(8,128)} async-done(((f32[64,3072]{1,0:T(8,128)}), f32[256,3072]{1,0:T(8,128)}) %all-gather.15.cloned.1.call-update) | async-done | bytes 3145744 | tf_op jit(solution)/shard_map/all_gather | solution.py:166
  492.0 3.5 fusion.74
  499.9 2.3 maximum_bitcast_fusion
  502.2 3.1 stack_reshape.6
  505.3 16.8 %all-gather.17.cloned.1.call-done = f32[256,3072]{1,0:T(8,128)} async-done(((f32[64,3072]{1,0:T(8,128)}), f32[256,3072]{1,0:T(8,128)}) %all-gather.17.cloned.1.call-update) | async-done | bytes 3145744 | tf_op jit(solution)/shard_map/all_gather | solution.py:166
  522.2 4.0 fusion.75
  528.2 1.9 fusion.59
  530.1 2.5 stack.36
  532.6 3.6 copy.27
  536.3 15.9 %all-gather.19.cloned.1.call-done = f32[256,3072]{1,0:T(8,128)} async-done(((f32[64,3072]{1,0:T(8,128)}), f32[256,3072]{1,0:T(8,128)}) %all-gather.19.cloned.1.call-update) | async-done | bytes 3145744 | tf_op jit(solution)/shard_map/all_gather | solution.py:166
  552.1 3.5 fusion.76
  560.0 3.8 maximum_bitcast_fusion.1
  563.8 3.0 stack_reshape.7
  566.8 2.7 pad_maximum_fusion.6.u_ref
  569.5 45.7 %shard_map.59 = f32[2,512,128]{2,1,0:T(8,128)} custom-call(f32[2,512,512]{2,1,0:T(8,128)} %pad_maximum_fusion.6.u_ref, f32[2,512,128]{2,1,0:T(8,128)} %jj_ref.1), custom_call_target="tpu_custom_call" | custom-call | tf_op jit(solution)/shard_map/pallas_call | solution.py:109
  615.2 1.9 copy.31
  (120 shorter events, 28.2 us)
Async XLA Ops:
  7.2 71.4 %all-gather.21.cloned.1.call-start = ((), (), s32[]{:S(2)}) async-start(), calls=%async_computation.12 | async-start | bytes 3932160 | tf_op jit(solution)/shard_map/all_gather | solution.py:159
  15.3 127.1 %all-gather.23.cloned.1.call-start = ((), (), s32[]{:S(2)}) async-start(), calls=%async_computation.13 | async-start | bytes 3932160 | tf_op jit(solution)/shard_map/all_gather | solution.py:159
  16.0 190.1 %all-gather.25.cloned.1.call-start = ((), (), s32[]{:S(2)}) async-start(), calls=%async_computation.14 | async-start | bytes 3932160 | tf_op jit(solution)/shard_map/all_gather | solution.py:159
  16.7 253.0 %all-gather.27.cloned.1.call-start = ((), (), s32[]{:S(2)}) async-start(), calls=%async_computation.15 | async-start | bytes 3932160 | tf_op jit(solution)/shard_map/all_gather | solution.py:159
  17.3 25.8 %copy-start.28 = (s32[2,128]{1,0:T(2,128)S(1)}, s32[2,128]{1,0:T(2,128)}, u32[]{:S(2)}) copy-start(s32[2,128]{1,0:T(2,128)} %param.11) | copy-start | bytes 3076
  17.3 26.1 %copy-start.27 = (s32[3072]{0:T(1024)S(1)}, s32[3072]{0:T(1024)}, u32[]{:S(2)}) copy-start(s32[3072]{0:T(1024)} %constant.204) | copy-start | bytes 36868
  17.3 291.8 %reduce-scatter.5.cloned.1.call-start = ((), (), s32[]{:S(2)}) async-start(), calls=%async_computation.4 | async-start | bytes 3932160 | tf_op jit(solution)/shard_map/reduce_scatter | solution.py:164
  81.0 1.2 copy-start.5
  81.1 1.7 copy-start.7
  114.6 235.1 %reduce-scatter.7.cloned.1.call-start = ((), (), s32[]{:S(2)}) async-start(), calls=%async_computation.5 | async-start | bytes 3932160 | tf_op jit(solution)/shard_map/reduce_scatter | solution.py:164
  144.8 1.2 copy-start.13
  144.8 1.7 copy-start.16
  178.6 211.6 %reduce-scatter.9.cloned.1.call-start = ((), (), s32[]{:S(2)}) async-start(), calls=%async_computation.6 | async-start | bytes 3932160 | tf_op jit(solution)/shard_map/reduce_scatter | solution.py:164
  208.5 1.2 copy-start.9
  208.6 1.7 copy-start.11
  242.0 189.5 %reduce-scatter.11.cloned.1.call-start = ((), (), s32[]{:S(2)}) async-start(), calls=%async_computation.7 | async-start | bytes 3932160 | tf_op jit(solution)/shard_map/reduce_scatter | solution.py:164
  272.2 1.1 copy-start.19
  272.2 1.6 copy-start.22
  305.9 156.1 %all-gather.13.cloned.1.call-start = ((), (), s32[]{:S(2)}) async-start(), calls=%async_computation.8 | async-start | bytes 3932160 | tf_op jit(solution)/shard_map/all_gather | solution.py:166
  311.3 122.3 %copy-start.2 = (f32[64,3072]{1,0:T(8,128)S(1)}, f32[64,3072]{1,0:T(8,128)}, u32[]{:S(2)}) copy-start(f32[64,3072]{1,0:T(8,128)} %neg.12) | copy-start | bytes 2359300
  311.3 180.7 %all-gather.15.cloned.1.call-start = ((), (), s32[]{:S(2)}) async-start(), calls=%async_computation.9 | async-start | bytes 3932160 | tf_op jit(solution)/shard_map/all_gather | solution.py:166
  351.8 81.8 %copy-start.3 = (f32[64,3072]{1,0:T(8,128)S(1)}, f32[64,3072]{1,0:T(8,128)}, u32[]{:S(2)}) copy-start(f32[64,3072]{1,0:T(8,128)} %neg.13) | copy-start | bytes 2359300
  351.8 170.3 %all-gather.17.cloned.1.call-start = ((), (), s32[]{:S(2)}) async-start(), calls=%async_computation.10 | async-start | bytes 3932160 | tf_op jit(solution)/shard_map/all_gather | solution.py:166
  392.3 42.5 %copy-start = (f32[64,3072]{1,0:T(8,128)S(1)}, f32[64,3072]{1,0:T(8,128)}, u32[]{:S(2)}) copy-start(f32[64,3072]{1,0:T(8,128)} %neg.14) | copy-start | bytes 2359300
  392.3 159.8 %all-gather.19.cloned.1.call-start = ((), (), s32[]{:S(2)}) async-start(), calls=%async_computation.11 | async-start | bytes 3932160 | tf_op jit(solution)/shard_map/all_gather | solution.py:166
  433.6 1.4 copy-start.1
  434.9 1.4 copy-start.4
  439.3 26.7 %copy-start.8 = (bf16[3072,256]{0,1:T(8,128)(2,1)S(1)}, bf16[3072,256]{0,1:T(8,128)(2,1)}, u32[]{:S(2)}) copy-start(bf16[3072,256]{0,1:T(8,128)(2,1)} %copy-done.7) | copy-start | bytes 4718596
  462.0 4.0 copy-start.17
  462.0 4.2 copy-start.32
  466.3 1.4 copy-start.6
  466.3 1.9 copy-start.14
  492.0 3.5 copy-start.18
  492.0 3.8 copy-start.31
  495.8 1.4 copy-start.15
  498.3 1.6 copy-start.26
  505.3 20.9 %copy-start.12 = (bf16[3072,256]{0,1:T(8,128)(2,1)S(1)}, bf16[3072,256]{0,1:T(8,128)(2,1)}, u32[]{:S(2)}) copy-start(bf16[3072,256]{0,1:T(8,128)(2,1)} %copy-done.11) | copy-start | bytes 4718596
  522.1 4.0 copy-start.23
  522.1 4.2 copy-start.30
  526.4 1.4 copy-start.10
  526.4 1.9 copy-start.20
  552.1 3.5 copy-start.24
  552.1 3.8 copy-start.29
  555.9 1.4 copy-start.21
  560.0 6.8 %copy-start.25 = (f32[1,512,512]{2,1,0:T(8,128)S(1)}, f32[1,512,512]{2,1,0:T(8,128)}, u32[]{:S(2)}) copy-start(f32[1,512,512]{2,1,0:T(8,128)} %stack_reshape.6) | copy-start | bytes 3145732
Sparse Core Ops, SparseCore 0:
  15.4 63.1 all-gather.20
  80.1 62.1 all-gather.22
  143.9 62.1 all-gather.24
  207.5 62.1 all-gather.26
  272.1 37.0 reduce-scatter.4
  311.7 37.9 reduce-scatter.6
  352.2 37.9 reduce-scatter.8
  393.5 37.9 reduce-scatter.10
  433.1 28.9 all-gather.12
  463.4 28.5 all-gather.14
  493.6 28.5 all-gather.16
  523.6 28.5 all-gather.18

commit v3 on v2

--- a/solution.py
+++ b/solution.py
@@ -120,6 +120,71 @@
         ],
         compiler_params=pltpu.CompilerParams(collective_id=0, has_side_effects=True),
     )(update, jj_inverse)
+
+
+def product_kernel(a_ref, b_ref, scale_ref, out_ref, bh_ref, bl_ref):
+    @pl.when(pl.program_id(0) == 0)
+    def _():
+        b = b_ref[...]
+        high = b.astype(jnp.bfloat16)
+        bh_ref[...] = high
+        bl_ref[...] = (b - high.astype(jnp.float32)).astype(jnp.bfloat16)
+
+    a = a_ref[...]
+    ah = a.astype(jnp.bfloat16)
+    al = (a - ah.astype(jnp.float32)).astype(jnp.bfloat16)
+    total = jnp.dot(ah, bh_ref[...], preferred_element_type=jnp.float32)
+    total += jnp.dot(ah, bl_ref[...], preferred_element_type=jnp.float32)
+    total += jnp.dot(al, bh_ref[...], preferred_element_type=jnp.float32)
+    out_ref[...] = total.T * scale_ref[...]
+
+
+def product(a, b, scale):
+    rows, depth = a.shape
+    columns = b.shape[1]
+    tile = 256 if rows % 256 == 0 else rows
+    return pl.pallas_call(
+        product_kernel,
+        grid=(rows // tile,),
+        out_shape=jax.ShapeDtypeStruct((columns, rows), jnp.float32),
+        in_specs=[
+            pl.BlockSpec((tile, depth), lambda i: (i, 0)),
+            pl.BlockSpec((depth, columns), lambda i: (0, 0)),
+            pl.BlockSpec((1, tile), lambda i: (0, i)),
+        ],
+        out_specs=pl.BlockSpec((columns, tile), lambda i: (0, i)),
+        scratch_shapes=[pltpu.VMEM((depth, columns), jnp.bfloat16)] * 2,
+        compiler_params=pltpu.CompilerParams(vmem_limit_bytes=40 * 1024 * 1024),
+        cost_estimate=pl.CostEstimate(
+            flops=6 * rows * depth * columns, bytes_accessed=4 * rows * depth, transcendentals=0
+        ),
+    )(a, b, scale)
+
+
+def swap(value, distance):
+    return lax.ppermute(value, "col", [(i, i ^ distance) for i in range(lax.axis_size("col"))])
+
+
+def scatter_sum(partial, col_index):
+    if lax.axis_size("col") != 4:
+        return lax.psum_scatter(partial, "col", scatter_dimension=0, tiled=True)
+    pieces = partial.reshape(2, 2, partial.shape[0] // 4, partial.shape[1])
+    far, near = col_index // 2, col_index % 2
+    sent = lax.dynamic_index_in_dim(pieces, 1 - near, 1, keepdims=False)
+    summed = lax.dynamic_index_in_dim(pieces, near, 1, keepdims=False) + swap(sent, 1)
+    sent = lax.dynamic_index_in_dim(summed, 1 - far, 0, keepdims=False)
+    return lax.dynamic_index_in_dim(summed, far, 0, keepdims=False) + swap(sent, 2)
+
+
+def widen(own, col_index):
+    if lax.axis_size("col") != 4:
+        return lax.all_gather(own, "col", axis=0, tiled=True)
+    far, near = col_index // 2, col_index % 2
+    other = swap(own, 2)
+    pair = jnp.stack([jnp.where(far == 0, own, other), jnp.where(far == 0, other, own)])
+    across = swap(pair, 1)
+    wide = jnp.stack([jnp.where(near == 0, pair, across), jnp.where(near == 0, across, pair)], axis=1)
+    return wide.reshape(4 * own.shape[0], own.shape[1])
 
 
 def shards(sigma_anc, normal_factor, jj_inverse, blocks):
@@ -143,30 +208,37 @@
     root_col = start_row // tile_cols
     square = tile_rows == tile_cols
     offset = jnp.clip(start_row - col_index * tile_cols, 0, tile_cols - tile_rows)
-    ah, al = split(sigma_anc)
-    a3 = jnp.concatenate([ah, ah, al], axis=1)
 
     def slab_of(value):
         return value if square else lax.dynamic_slice_in_dim(value, offset, tile_rows, 0)
 
+    order = [(supernode, half) for supernode in range(supernodes) for half in range(HALVES)]
+    own_list = []
+    wide_list = []
+    slab_list = []
+    for at, (supernode, half) in enumerate(order):
+        local = chunks[supernode, half]
+        if at >= 2:
+            local, own_list[at - 2] = lax.optimization_barrier((local, own_list[at - 2]))
+        gathered = lax.all_gather(local, "row", axis=0, tiled=True)
+        if at >= 2:
+            gathered, own_list[at - 1], wide_list[at - 2] = lax.optimization_barrier(
+                (gathered, own_list[at - 1], wide_list[at - 2])
+            )
+        elif at >= 1:
+            gathered, own_list[at - 1] = lax.optimization_barrier((gathered, own_list[at - 1]))
+        own_list.append(scatter_sum(product(sigma_anc, gathered, -row_mask[supernode][None, :]), col_index))
+        wide_list.append(widen(own_list[at], col_index))
+        slab_list.append(split(slab_of(gathered)))
     rj_list = []
     update_list = []
     for supernode in range(supernodes):
-        own_list = []
-        wide_list = []
-        gathered_list = []
-        for half in range(HALVES):
-            gathered = lax.all_gather(chunks[supernode, half], "row", axis=0, tiled=True)
-            bh, bl = split(gathered)
-            gathered_list.append((slab_of(bh), slab_of(bl)))
-            b3 = jnp.concatenate([bh, bl, bh], axis=0)
-            partial = lax.dot_general(b3, a3, (((0,), (1,)), ((), ())), preferred_element_type=jnp.float32)
-            own = -lax.psum_scatter(partial * row_mask[supernode][None, :], "col", scatter_dimension=0, tiled=True)
-            own_list.append(own)
-            wide_list.append(split(lax.all_gather(own, "col", axis=0, tiled=True)))
-        rj_list.append(jnp.concatenate(own_list, axis=0).T)
-        slab = tuple(jnp.concatenate([g[i] for g in gathered_list], axis=1) for i in range(2))
-        update = jnp.stack([dot3(slab, wide, ((0,), (1,))) for wide in wide_list], axis=1)
+        own = own_list[HALVES * supernode:HALVES * (supernode + 1)]
+        rj_list.append(jnp.concatenate(own, axis=0).T)
+        pieces = slab_list[HALVES * supernode:HALVES * (supernode + 1)]
+        slab = tuple(jnp.concatenate([piece[i] for piece in pieces], axis=1) for i in range(2))
+        wides = wide_list[HALVES * supernode:HALVES * (supernode + 1)]
+        update = jnp.stack([dot3(slab, split(wide), ((0,), (1,))) for wide in wides], axis=1)
         update = update.reshape(HALVES, col_count, sub, HALVES, col_count, sub).transpose(1, 0, 2, 4, 3, 5)
         update_list.append(update.reshape(w, w))
     update = jnp.stack(update_list)

time: 632 us -> 510 us (0.81)
  matrix products: 152 us -> 19.8 us
  waiting for transfers between devices: 301 us -> 201 us
  Pallas kernels: 45.7 us -> 133 us
  local copies, waits for them, and re-layouts: 52.1 us -> 72.9 us
  other arithmetic: 57.6 us -> 47 us
  starting transfers between devices: 0.7 us -> 10.9 us
    dot_general x4 -> x0, matrix products: 127 us -> none  [shards(): lax.dot_general(b3, a3, (((0,), (1,)), ((), ())), preferred_element_type=...]
    reduce_scatter x4 -> x0, waiting for transfers between devices: 119 us -> none  [shards(): lax.psum_scatter(partial * row_mask[supernode][None, :], 'col', scatter_d...]
    ppermute x0 -> x16, waiting for transfers between devices: none -> 109 us  [swap(): lax.ppermute(value, 'col', [(i, i ^ distance) for i in range(lax.axis_siz...]
    pallas_call x0 -> x4, Pallas kernels: none -> 91.2 us  [product(): pl.pallas_call(product_kernel, grid=(rows // tile,), out_shape=jax.ShapeD...]
    all_gather x8 -> x4, waiting for transfers between devices: 180 us -> 91.8 us  [shards(): gathered = lax.all_gather(local, 'row', axis=0, tiled=True)]
    convert_element_type x5 -> x4, other arithmetic: 35.5 us -> 7.96 us  [split(): return (high.astype(jnp.bfloat16), (value - high).astype(jnp.bfloat16))]
    another operation x0 -> x16, other arithmetic: none -> 16 us  [the longest x8 8.67 us: widen(): jnp.stack([jnp.where(near == 0, pair, across), jnp.where(near == 0, acros...]
    unnamed x69 -> x97, local copies, waits for them, and re-layouts: 17.4 us -> 32.3 us
  transfers between devices with their start and end apart: 12 -> 20, of which waited for: 12 -> 12; matrix products, arithmetic and copies ran while one was open for 36% -> 18% of each run, Pallas kernels for 0% -> 14%
where the time goes in v3:
time: 510 us; the launch traced here: 500 us
  waiting for transfers between devices  201 us (39%)
  Pallas kernels  133 us (26%)
  local copies, waits for them, and re-layouts  72.9 us (14%)
  other arithmetic  47 us (9%)
  matrix products  19.8 us (4%)
  between operations  15.1 us (3%)
  starting transfers between devices  10.9 us (2%)
    ppermute x16, waiting for transfers between devices, swap(): lax.ppermute(value, 'col', [(i, i ^ distance) for i in range(lax.axis_siz...  109 us
    all_gather x4, waiting for transfers between devices, shards(): gathered = lax.all_gather(local, 'row', axis=0, tiled=True)  91.8 us
    pallas_call x4, Pallas kernels, product(): pl.pallas_call(product_kernel, grid=(rows // tile,), out_shape=jax.ShapeD...  91.2 us
    pallas_call x1, Pallas kernels, finish_diagonal(): pl.pallas_call(functools.partial(diagonal_kernel, n), out_shape=jax.Shape...  42.2 us
    unnamed x97, local copies, waits for them, and re-layouts  32.3 us
    dot_general x12, matrix products, dot(): lax.dot_general(a, b, (dims, ((), ())), preferred_element_type=jnp.float32)  19.8 us
    another operation x8, local copies, waits for them, and re-layouts, shards(): jnp.stack([dot3(slab, split(wide), ((0,), (1,))) for wide in wides], axis=1)  14.8 us
    ppermute x16, starting transfers between devices, swap(): lax.ppermute(value, 'col', [(i, i ^ distance) for i in range(lax.axis_siz...  10.7 us
  transfers between devices with their start and end apart: 20, of which 12 were waited for; matrix products, arithmetic and copies ran while one was open for 18% of the time, Pallas kernels for 14%

profile of v3, /device:TPU:19, one launch (start us, length us, event | category | flops | bytes accessed | tf_op | source)
XLA Modules:
  0.0 500.3 jit_solution(3471784641670071542)
XLA Ops:
  10.6 2.4 copy.40
  17.8 8.1 %gather_fusion.1 = f32[3072,2]{1,0:T(8,128)S(1)} fusion(f32[2,64]{0,1:T(8,128)S(1)} %copy.45, s32[3072]{0:T(1024)S(1)} %broadcast_clamp_fusion), kind=kCustom, calls=%fused_computation.1 | custom fusion | bytes 61440 | tf_op jit(solution)/shard_map/jit(_take)/gather | solution.py:18
  26.4 53.1 %all-gather.13.cloned.1.call-done = f32[1,1,3072,256]{3,2,1,0:T(8,128)} async-done(((f32[1,1,768,256]{3,2,1,0:T(8,128)}), f32[1,1,3072,256]{3,2,1,0:T(8,128)}) %all-gather.13.cloned.1.call-update) | async-done | bytes 3145744 | tf_op jit(solution)/shard_map/all_gather | solution.py:223
  79.6 1.9 copy-done
  81.5 22.9 %shard_map.59 = f32[256,3072]{1,0:T(8,128)S(1)} custom-call(f32[3072,3072]{1,0:T(8,128)} %a_ref.7, f32[3072,256]{1,0:T(8,128)S(1)} %bitcast.132, f32[1,3072]{1,0:T(1,128)S(1)} %get-tuple-element.87.scale_ref), custom_call_target="tpu_custom_call" | custom-call | flops 14495514624 | bytes 37748736 | tf_op jit(solution)/shard_map/pallas_call | solution.py:146
  106.3 3.4 collective-permute-done
  112.9 18.6 %collective-permute-done.1 = f32[64,3072]{1,0:T(8,128)S(1)} collective-permute-done((f32[64,3072]{1,0:T(8,128)S(1)}, f32[64,3072]{1,0:T(8,128)S(1)}, u32[]{:S(2)}, u32[]{:S(2)}) %collective-permute-start.1) | collective-permute-done | bytes 786464 | tf_op jit(solution)/shard_map/ppermute | solution.py:165
  131.4 2.1 bitcast_add_fusion.7
  133.9 9.5 %all-gather.11.cloned.1.call-done = f32[1,1,3072,256]{3,2,1,0:T(8,128)} async-done(((f32[1,1,768,256]{3,2,1,0:T(8,128)}), f32[1,1,3072,256]{3,2,1,0:T(8,128)}) %all-gather.11.cloned.1.call-update) | async-done | bytes 3145744 | tf_op jit(solution)/shard_map/all_gather | solution.py:223
  143.3 1.9 copy-done.2
  145.2 22.6 %shard_map.60 = f32[256,3072]{1,0:T(8,128)S(1)} custom-call(f32[3072,3072]{1,0:T(8,128)} %a_ref.7, f32[3072,256]{1,0:T(8,128)S(1)} %bitcast.133, f32[1,3072]{1,0:T(1,128)S(1)} %get-tuple-element.87.scale_ref), custom_call_target="tpu_custom_call" | custom-call | flops 14495514624 | bytes 37748736 | tf_op jit(solution)/shard_map/pallas_call | solution.py:146
  169.7 2.3 copy.65
  172.0 2.3 copy.70
  179.5 3.5 fusion
  183.1 13.8 %collective-permute-done.3 = f32[64,3072]{1,0:T(8,128)S(1)} collective-permute-done((f32[64,3072]{1,0:T(8,128)S(1)}, f32[64,3072]{1,0:T(8,128)S(1)}, u32[]{:S(2)}, u32[]{:S(2)}) %collective-permute-start.3) | collective-permute-done | bytes 786464 | tf_op jit(solution)/shard_map/ppermute | solution.py:165
  197.6 1.9 pad_maximum_fusion
  199.5 15.5 %collective-permute-done.8 = f32[64,3072]{1,0:T(8,128)S(1)} collective-permute-done((f32[64,3072]{1,0:T(8,128)S(1)}, f32[64,3072]{1,0:T(8,128)S(1)}, u32[]{:S(2)}, u32[]{:S(2)}) %collective-permute-start.8) | collective-permute-done | bytes 786464 | tf_op jit(solution)/shard_map/ppermute | solution.py:165
  216.3 19.8 %all-gather.7.cloned.1.call-done.b_ref = f32[3072,256]{1,0:T(8,128)} async-done(((f32[768,256]{1,0:T(8,128)}), f32[3072,256]{1,0:T(8,128)}) %all-gather.7.cloned.1.call-update) | async-done | bytes 3145744 | tf_op jit(solution)/shard_map/all_gather | solution.py:223
  236.2 1.9 copy-done.4
  238.1 23.0 %shard_map.61 = f32[256,3072]{1,0:T(8,128)S(1)} custom-call(f32[3072,3072]{1,0:T(8,128)} %a_ref.7, f32[3072,256]{1,0:T(8,128)S(1)} %copy-done.4, f32[1,3072]{1,0:T(1,128)S(1)} %get-tuple-element.86.scale_ref), custom_call_target="tpu_custom_call" | custom-call | flops 14495514624 | bytes 37748736 | tf_op jit(solution)/shard_map/pallas_call | solution.py:146
  266.7 1.8 fusion.20
  268.6 4.7 fusion.16
  273.3 2.4 stack.117
  275.8 3.4 copy.58
  283.9 15.6 %collective-permute-done.7 = f32[64,3072]{1,0:T(8,128)S(1)} collective-permute-done((f32[64,3072]{1,0:T(8,128)S(1)}, f32[64,3072]{1,0:T(8,128)S(1)}, u32[]{:S(2)}, u32[]{:S(2)}) %collective-permute-start.7) | collective-permute-done | bytes 786464 | tf_op jit(solution)/shard_map/ppermute | solution.py:165
  301.5 3.0 maximum_bitcast_fusion.2
  304.4 13.0 %collective-permute-done.12 = f32[64,3072]{1,0:T(8,128)S(1)} collective-permute-done((f32[64,3072]{1,0:T(8,128)S(1)}, f32[64,3072]{1,0:T(8,128)S(1)}, u32[]{:S(2)}, u32[]{:S(2)}) %collective-permute-start.12) | collective-permute-done | bytes 786464 | tf_op jit(solution)/shard_map/ppermute | solution.py:165
  319.3 2.2 collective-permute-start.13
  321.5 9.3 %all-gather.9.cloned.1.call-done.b_ref = f32[3072,256]{1,0:T(8,128)} async-done(((f32[768,256]{1,0:T(8,128)}), f32[3072,256]{1,0:T(8,128)}) %all-gather.9.cloned.1.call-update) | async-done | bytes 3145744 | tf_op jit(solution)/shard_map/all_gather | solution.py:223
  330.9 3.1 fusion.27
  335.9 22.7 %shard_map.62 = f32[256,3072]{1,0:T(8,128)S(1)} custom-call(f32[3072,3072]{1,0:T(8,128)} %a_ref.7, f32[3072,256]{1,0:T(8,128)S(1)} %copy-done.6, f32[1,3072]{1,0:T(1,128)S(1)} %get-tuple-element.86.scale_ref), custom_call_target="tpu_custom_call" | custom-call | flops 14495514624 | bytes 37748736 | tf_op jit(solution)/shard_map/pallas_call | solution.py:146
  361.1 3.4 fusion.4
  364.5 1.8 fusion.17
  366.3 2.4 stack.118
  368.7 2.4 copy.59
  371.1 3.6 maximum_bitcast_fusion
  374.7 4.3 stack_reshape.6
  384.5 14.8 %collective-permute-done.11 = f32[64,3072]{1,0:T(8,128)S(1)} collective-permute-done((f32[64,3072]{1,0:T(8,128)S(1)}, f32[64,3072]{1,0:T(8,128)S(1)}, u32[]{:S(2)}, u32[]{:S(2)}) %collective-permute-start.11) | collective-permute-done | bytes 786464 | tf_op jit(solution)/shard_map/ppermute | solution.py:165
  402.3 14.7 %collective-permute-done.14 = f32[64,3072]{1,0:T(8,128)S(1)} collective-permute-done((f32[64,3072]{1,0:T(8,128)S(1)}, f32[64,3072]{1,0:T(8,128)S(1)}, u32[]{:S(2)}, u32[]{:S(2)}) %collective-permute-start.14) | collective-permute-done | bytes 786464 | tf_op jit(solution)/shard_map/ppermute | solution.py:165
  418.8 2.5 collective-permute-start.15
  424.7 2.1 copy.62
  428.4 2.6 copy.64
  431.0 2.1 select_bitcast_fusion.1
  441.2 2.3 maximum_bitcast_fusion.1
  443.5 3.0 stack_reshape.7
  446.5 2.7 pad_maximum_fusion.9.u_ref
  449.2 42.2 %shard_map.63 = f32[2,512,128]{2,1,0:T(8,128)} custom-call(f32[2,512,512]{2,1,0:T(8,128)} %pad_maximum_fusion.9.u_ref, f32[2,512,128]{2,1,0:T(8,128)} %jj_ref.1), custom_call_target="tpu_custom_call" | custom-call | tf_op jit(solution)/shard_map/pallas_call | solution.py:109
  491.5 1.9 copy.78
  (183 shorter events, 64.5 us)
Async XLA Ops:
  7.2 72.4 %all-gather.13.cloned.1.call-start = ((), (), s32[]{:S(2)}) async-start(), calls=%async_computation.3 | async-start | bytes 3932160 | tf_op jit(solution)/shard_map/all_gather | solution.py:223
  16.2 127.2 %all-gather.11.cloned.1.call-start = ((), (), s32[]{:S(2)}) async-start(), calls=%async_computation.2 | async-start | bytes 3932160 | tf_op jit(solution)/shard_map/all_gather | solution.py:223
  17.4 218.8 %all-gather.7.cloned.1.call-start = ((), (), s32[]{:S(2)}) async-start(), calls=%async_computation | async-start | bytes 3932160 | tf_op jit(solution)/shard_map/all_gather | solution.py:223
  79.6 1.9 copy-start
  105.7 4.0 collective-permute-start
  112.5 18.9 %collective-permute-start.1 = (f32[64,3072]{1,0:T(8,128)S(1)}, f32[64,3072]{1,0:T(8,128)S(1)}, u32[]{:S(2)}, u32[]{:S(2)}) collective-permute-start(f32[64,3072]{1,0:T(8,128)S(1)} %dynamic-slice_bitcast_fusion.7), channel_id=1, source_target_pairs={{0,2},{1,3},{2,0},{3,1},{4,6},{5,7},{6,4},{7,5},{8,10},{9,11},{10,... | collective-permute-start | bytes 2359304 | tf_op jit(solution)/shard_map/ppermute | solution.py:165
  133.6 40.9 %collective-permute-start.4 = (f32[64,3072]{1,0:T(8,128)}, f32[64,3072]{1,0:T(8,128)}, u32[]{:S(2)}, u32[]{:S(2)}) collective-permute-start(f32[64,3072]{1,0:T(8,128)} %bitcast_add_fusion.7), channel_id=1, source_target_pairs={{0,2},{1,3},{2,0},{3,1},{4,6},{5,7},{6,4},{7,5},{8,10},{9,11},{10,... | collective-permute-start | bytes 2359304 | tf_op jit(solution)/shard_map/ppermute | solution.py:165
  143.3 1.9 copy-start.2
  169.1 7.1 %collective-permute-start.2 = (f32[2,64,3072]{2,1,0:T(8,128)}, f32[2,64,3072]{2,1,0:T(8,128)}, u32[]{:S(2)}, u32[]{:S(2)}) collective-permute-start(f32[2,64,3072]{2,1,0:T(8,128)} %dynamic-slice_bitcast_fusion.2), channel_id=1, source_target_pairs={{0,1},{1,0},{2,3},{3,2},{4,5},{5,4},{6,7},{7,6},{8,9},{9,8},{10,11... | collective-permute-start | bytes 4718600 | tf_op jit(solution)/shard_map/ppermute | solution.py:165
  174.4 156.5 %all-gather.9.cloned.1.call-start = ((), (), s32[]{:S(2)}) async-start(), calls=%async_computation.1 | async-start | bytes 3932160 | tf_op jit(solution)/shard_map/all_gather | solution.py:223
  176.1 21.2 %collective-permute-start.5 = (f32[2,64,3072]{2,1,0:T(8,128)S(1)}, f32[2,64,3072]{2,1,0:T(8,128)S(1)}, u32[]{:S(2)}, u32[]{:S(2)}) collective-permute-start(f32[2,64,3072]{2,1,0:T(8,128)S(1)} %pad_maximum_fusion.14), channel_id=1, source_target_pairs={{0,1},{1,0},{2,3},{3,2},{4,5},{5,4},{6,7},{7,6},{8,9},{9,8},{10,11... | collective-permute-start | bytes 4718600 | tf_op jit(solution)/shard_map/ppermute | solution.py:165
  176.2 2.4 copy-start.1
  176.2 3.3 copy-start.3
  178.0 18.8 %collective-permute-start.3 = (f32[64,3072]{1,0:T(8,128)S(1)}, f32[64,3072]{1,0:T(8,128)S(1)}, u32[]{:S(2)}, u32[]{:S(2)}) collective-permute-start(f32[64,3072]{1,0:T(8,128)S(1)} %dynamic-slice_bitcast_fusion.6), channel_id=1, source_target_pairs={{0,2},{1,3},{2,0},{3,1},{4,6},{5,7},{6,4},{7,5},{8,10},{9,11},{10,... | collective-permute-start | bytes 2359304 | tf_op jit(solution)/shard_map/ppermute | solution.py:165
  196.9 18.0 %copy-start.9 = (f32[64,3072]{1,0:T(8,128)}, f32[64,3072]{1,0:T(8,128)S(1)}, u32[]{:S(2)}) copy-start(f32[64,3072]{1,0:T(8,128)S(1)} %bitcast_add_fusion.6) | copy-start | bytes 2359300
  197.0 18.0 %collective-permute-start.8 = (f32[64,3072]{1,0:T(8,128)S(1)}, f32[64,3072]{1,0:T(8,128)S(1)}, u32[]{:S(2)}, u32[]{:S(2)}) collective-permute-start(f32[64,3072]{1,0:T(8,128)S(1)} %bitcast_add_fusion.6), channel_id=1, source_target_pairs={{0,2},{1,3},{2,0},{3,1},{4,6},{5,7},{6,4},{7,5},{8,10},{9,11},{10,... | collective-permute-start | bytes 2359304 | tf_op jit(solution)/shard_map/ppermute | solution.py:165
  236.2 1.9 copy-start.4
  238.1 26.9 %copy-start.33 = (bf16[3072,256]{1,0:T(8,128)(2,1)S(1)}, bf16[3072,256]{1,0:T(8,128)(2,1)}, u32[]{:S(2)}) copy-start(bf16[3072,256]{1,0:T(8,128)(2,1)} %get-tuple-element.90) | copy-start | bytes 4718596
  261.1 2.0 copy-start.15
  261.1 2.0 copy-start.17
  261.1 3.9 copy-start.31
  262.4 16.7 %collective-permute-start.6 = (f32[2,64,3072]{2,1,0:T(8,128)}, f32[2,64,3072]{2,1,0:T(8,128)}, u32[]{:S(2)}, u32[]{:S(2)}) collective-permute-start(f32[2,64,3072]{2,1,0:T(8,128)} %dynamic-slice_bitcast_fusion.1), channel_id=1, source_target_pairs={{0,1},{1,0},{2,3},{3,2},{4,5},{5,4},{6,7},{7,6},{8,9},{9,8},{10,11... | collective-permute-start | bytes 4718600 | tf_op jit(solution)/shard_map/ppermute | solution.py:165
  263.1 2.6 copy-start.28
  264.4 16.9 %collective-permute-start.9 = (f32[2,64,3072]{2,1,0:T(8,128)}, f32[2,64,3072]{2,1,0:T(8,128)}, u32[]{:S(2)}, u32[]{:S(2)}) collective-permute-start(f32[2,64,3072]{2,1,0:T(8,128)} %pad_maximum_fusion.15), channel_id=1, source_target_pairs={{0,1},{1,0},{2,3},{3,2},{4,5},{5,4},{6,7},{7,6},{8,9},{9,8},{10,11... | collective-permute-start | bytes 4718600 | tf_op jit(solution)/shard_map/ppermute | solution.py:165
  280.9 18.6 %collective-permute-start.7 = (f32[64,3072]{1,0:T(8,128)S(1)}, f32[64,3072]{1,0:T(8,128)S(1)}, u32[]{:S(2)}, u32[]{:S(2)}) collective-permute-start(f32[64,3072]{1,0:T(8,128)S(1)} %dynamic-slice_bitcast_fusion.5), channel_id=1, source_target_pairs={{0,2},{1,3},{2,0},{3,1},{4,6},{5,7},{6,4},{7,5},{8,10},{9,11},{10,... | collective-permute-start | bytes 2359304 | tf_op jit(solution)/shard_map/ppermute | solution.py:165
  299.6 17.8 %copy-start.7 = (f32[64,3072]{1,0:T(8,128)}, f32[64,3072]{1,0:T(8,128)S(1)}, u32[]{:S(2)}) copy-start(f32[64,3072]{1,0:T(8,128)S(1)} %bitcast_add_fusion.5) | copy-start | bytes 2359300
  299.6 17.8 %collective-permute-start.12 = (f32[64,3072]{1,0:T(8,128)S(1)}, f32[64,3072]{1,0:T(8,128)S(1)}, u32[]{:S(2)}, u32[]{:S(2)}) collective-permute-start(f32[64,3072]{1,0:T(8,128)S(1)} %bitcast_add_fusion.5), channel_id=1, source_target_pairs={{0,2},{1,3},{2,0},{3,1},{4,6},{5,7},{6,4},{7,5},{8,10},{9,11},{10,... | collective-permute-start | bytes 2359304 | tf_op jit(solution)/shard_map/ppermute | solution.py:165
  301.5 32.5 %copy-start.26 = (f32[2,2,64,3072]{3,2,1,0:T(8,128)}, f32[2,2,64,3072]{3,2,1,0:T(8,128)S(1)}, u32[]{:S(2)}) copy-start(f32[2,2,64,3072]{3,2,1,0:T(8,128)S(1)} %copy.55) | copy-start | bytes 9437188
  319.3 61.9 %collective-permute-start.13 = (f32[2,64,3072]{2,1,0:T(8,128)}, f32[2,64,3072]{2,1,0:T(8,128)}, u32[]{:S(2)}, u32[]{:S(2)}) collective-permute-start(f32[2,64,3072]{2,1,0:T(8,128)} %pad_maximum_fusion.16), channel_id=1, source_target_pairs={{0,1},{1,0},{2,3},{3,2},{4,5},{5,4},{6,7},{7,6},{8,9},{9,8},{10,11... | collective-permute-start | bytes 4718600 | tf_op jit(solution)/shard_map/ppermute | solution.py:165
  330.8 3.1 copy-start.32
  330.8 3.2 copy-start.34
  334.0 1.9 copy-start.6
  358.6 2.5 copy-start.5
  360.0 4.4 copy-start.27
  360.0 4.4 copy-start.29
  360.0 4.4 copy-start.30
  360.0 19.0 %collective-permute-start.10 = (f32[2,64,3072]{2,1,0:T(8,128)}, f32[2,64,3072]{2,1,0:T(8,128)}, u32[]{:S(2)}, u32[]{:S(2)}) collective-permute-start(f32[2,64,3072]{2,1,0:T(8,128)} %dynamic-slice_bitcast_fusion), channel_id=1, source_target_pairs={{0,1},{1,0},{2,3},{3,2},{4,5},{5,4},{6,7},{7,6},{8,9},{9,8},{10,11... | collective-permute-start | bytes 4718600 | tf_op jit(solution)/shard_map/ppermute | solution.py:165
  368.7 2.4 copy-start.24
  380.8 18.5 %collective-permute-start.11 = (f32[64,3072]{1,0:T(8,128)S(1)}, f32[64,3072]{1,0:T(8,128)S(1)}, u32[]{:S(2)}, u32[]{:S(2)}) collective-permute-start(f32[64,3072]{1,0:T(8,128)S(1)} %dynamic-slice_bitcast_fusion.4), channel_id=1, source_target_pairs={{0,2},{1,3},{2,0},{3,1},{4,6},{5,7},{6,4},{7,5},{8,10},{9,11},{10,... | collective-permute-start | bytes 2359304 | tf_op jit(solution)/shard_map/ppermute | solution.py:165
  399.4 1.9 copy-start.41
  399.4 17.6 %collective-permute-start.14 = (f32[64,3072]{1,0:T(8,128)S(1)}, f32[64,3072]{1,0:T(8,128)S(1)}, u32[]{:S(2)}, u32[]{:S(2)}) collective-permute-start(f32[64,3072]{1,0:T(8,128)S(1)} %bitcast_add_fusion.4), channel_id=1, source_target_pairs={{0,2},{1,3},{2,0},{3,1},{4,6},{5,7},{6,4},{7,5},{8,10},{9,11},{10,... | collective-permute-start | bytes 2359304 | tf_op jit(solution)/shard_map/ppermute | solution.py:165
  417.1 1.7 copy-start.20
  418.8 12.2 %collective-permute-start.15 = (f32[2,64,3072]{2,1,0:T(8,128)}, f32[2,64,3072]{2,1,0:T(8,128)}, u32[]{:S(2)}, u32[]{:S(2)}) collective-permute-start(f32[2,64,3072]{2,1,0:T(8,128)} %pad_maximum_fusion.17), channel_id=1, source_target_pairs={{0,1},{1,0},{2,3},{3,2},{4,5},{5,4},{6,7},{7,6},{8,9},{9,8},{10,11... | collective-permute-start | bytes 4718600 | tf_op jit(solution)/shard_map/ppermute | solution.py:165
  421.3 1.9 copy-start.37
  424.2 2.6 copy-start.8
  433.8 1.9 copy-start.42
  436.7 1.9 copy-start.38
  443.5 3.0 copy-start.23
  (17 other events, 23.4 us)
Sparse Core Ops, SparseCore 0:
  16.3 63.2 all-gather.12
  81.1 62.1 all-gather.10
  174.5 61.6 all-gather.6
  268.7 62.0 all-gather.8

commit v4 on v3

--- a/solution.py
+++ b/solution.py
@@ -218,8 +218,6 @@
     slab_list = []
     for at, (supernode, half) in enumerate(order):
         local = chunks[supernode, half]
-        if at >= 2:
-            local, own_list[at - 2] = lax.optimization_barrier((local, own_list[at - 2]))
         gathered = lax.all_gather(local, "row", axis=0, tiled=True)
         if at >= 2:
             gathered, own_list[at - 1], wide_list[at - 2] = lax.optimization_barrier(

time: 510 us -> 457 us (0.90)
  waiting for transfers between devices: 201 us -> 148 us
    ppermute x16, waiting for transfers between devices: 109 us -> 76.7 us  [swap(): lax.ppermute(value, 'col', [(i, i ^ distance) for i in range(lax.axis_siz...]
    all_gather x4, waiting for transfers between devices: 91.8 us -> 71.4 us  [shards(): gathered = lax.all_gather(local, 'row', axis=0, tiled=True)]
    unnamed x97 -> x93, local copies, waits for them, and re-layouts: 32.3 us -> 29.7 us
  transfers between devices with their start and end apart: 20 -> 20, of which waited for: 12 -> 9; matrix products, arithmetic and copies ran while one was open for 18% -> 21% of each run, Pallas kernels for 14% -> 20%
where the time goes in v4:
time: 457 us; the launch traced here: 451 us
  waiting for transfers between devices  148 us (32%)
  Pallas kernels  137 us (30%)
  local copies, waits for them, and re-layouts  70.2 us (15%)
  other arithmetic  51.3 us (11%)
  matrix products  16.1 us (4%)
  between operations  14.9 us (3%)
  starting transfers between devices  13.1 us (3%)
    pallas_call x4, Pallas kernels, product(): pl.pallas_call(product_kernel, grid=(rows // tile,), out_shape=jax.ShapeD...  92.2 us
    ppermute x16, waiting for transfers between devices, swap(): lax.ppermute(value, 'col', [(i, i ^ distance) for i in range(lax.axis_siz...  76.7 us
    all_gather x4, waiting for transfers between devices, shards(): gathered = lax.all_gather(local, 'row', axis=0, tiled=True)  71.4 us
    pallas_call x1, Pallas kernels, finish_diagonal(): pl.pallas_call(functools.partial(diagonal_kernel, n), out_shape=jax.Shape...  44.9 us
    unnamed x93, local copies, waits for them, and re-layouts  29.7 us
    dot_general x12, matrix products, dot(): lax.dot_general(a, b, (dims, ((), ())), preferred_element_type=jnp.float32)  16.1 us
    another operation x8, local copies, waits for them, and re-layouts, shards(): jnp.stack([dot3(slab, split(wide), ((0,), (1,))) for wide in wides], axis=1)  14.7 us
    ppermute x16, starting transfers between devices, swap(): lax.ppermute(value, 'col', [(i, i ^ distance) for i in range(lax.axis_siz...  12.7 us
  transfers between devices with their start and end apart: 20, of which 9 were waited for; matrix products, arithmetic and copies ran while one was open for 21% of the time, Pallas kernels for 20%

profile of v4, /device:TPU:19, one launch (start us, length us, event | category | flops | bytes accessed | tf_op | source)
XLA Modules:
  0.0 450.9 jit_solution(9905901671059130435)
XLA Ops:
  10.6 2.4 copy.40
  17.8 8.1 %gather_fusion.1 = f32[3072,2]{1,0:T(8,128)S(1)} fusion(f32[2,64]{0,1:T(8,128)S(1)} %copy.44, s32[3072]{0:T(1024)S(1)} %broadcast_clamp_fusion), kind=kCustom, calls=%fused_computation.1 | custom fusion | bytes 61440 | tf_op jit(solution)/shard_map/jit(_take)/gather | solution.py:18
  26.4 53.1 %all-gather.11.cloned.1.call-done = f32[1,1,3072,256]{3,2,1,0:T(8,128)} async-done(((f32[1,1,768,256]{3,2,1,0:T(8,128)}), f32[1,1,3072,256]{3,2,1,0:T(8,128)}) %all-gather.11.cloned.1.call-update) | async-done | bytes 3145744 | tf_op jit(solution)/shard_map/all_gather | solution.py:221
  79.5 1.9 copy-done.2
  81.4 22.9 %shard_map.59 = f32[256,3072]{1,0:T(8,128)S(1)} custom-call(f32[3072,3072]{1,0:T(8,128)} %a_ref.7, f32[3072,256]{1,0:T(8,128)S(1)} %bitcast.134, f32[1,3072]{1,0:T(1,128)S(1)} %get-tuple-element.79.scale_ref), custom_call_target="tpu_custom_call" | custom-call | flops 14495514624 | bytes 37748736 | tf_op jit(solution)/shard_map/pallas_call | solution.py:146
  106.3 2.3 copy.69
  112.8 18.6 %collective-permute-done.1 = f32[64,3072]{1,0:T(8,128)S(1)} collective-permute-done((f32[64,3072]{1,0:T(8,128)S(1)}, f32[64,3072]{1,0:T(8,128)S(1)}, u32[]{:S(2)}, u32[]{:S(2)}) %collective-permute-start.1) | collective-permute-done | bytes 786464 | tf_op jit(solution)/shard_map/ppermute | solution.py:165
  131.4 2.1 bitcast_add_fusion.7
  133.8 9.5 %all-gather.9.cloned.1.call-done = f32[1,1,3072,256]{3,2,1,0:T(8,128)} async-done(((f32[1,1,768,256]{3,2,1,0:T(8,128)}), f32[1,1,3072,256]{3,2,1,0:T(8,128)}) %all-gather.9.cloned.1.call-update) | async-done | bytes 3145744 | tf_op jit(solution)/shard_map/all_gather | solution.py:221
  143.3 1.9 copy-done.4
  145.2 23.0 %shard_map.60 = f32[256,3072]{1,0:T(8,128)S(1)} custom-call(f32[3072,3072]{1,0:T(8,128)} %a_ref.7, f32[3072,256]{1,0:T(8,128)S(1)} %bitcast.135, f32[1,3072]{1,0:T(1,128)S(1)} %get-tuple-element.79.scale_ref), custom_call_target="tpu_custom_call" | custom-call | flops 14495514624 | bytes 37748736 | tf_op jit(solution)/shard_map/pallas_call | solution.py:146
  170.0 2.3 copy.72
  174.1 1.8 bitcast_add_fusion.2
  177.4 3.5 fusion
  180.9 13.9 %collective-permute-done.3 = f32[64,3072]{1,0:T(8,128)S(1)} collective-permute-done((f32[64,3072]{1,0:T(8,128)S(1)}, f32[64,3072]{1,0:T(8,128)S(1)}, u32[]{:S(2)}, u32[]{:S(2)}) %collective-permute-start.3) | collective-permute-done | bytes 786464 | tf_op jit(solution)/shard_map/ppermute | solution.py:165
  196.3 1.9 pad_maximum_fusion
  198.2 8.8 %all-gather.13.cloned.1.call-done = f32[1,1,3072,256]{3,2,1,0:T(8,128)} async-done(((f32[1,1,768,256]{3,2,1,0:T(8,128)}), f32[1,1,3072,256]{3,2,1,0:T(8,128)}) %all-gather.13.cloned.1.call-update) | async-done | bytes 3145744 | tf_op jit(solution)/shard_map/all_gather | solution.py:221
  207.0 1.9 copy-done
  208.9 23.6 %shard_map.61 = f32[256,3072]{1,0:T(8,128)S(1)} custom-call(f32[3072,3072]{1,0:T(8,128)} %a_ref.7, f32[3072,256]{1,0:T(8,128)S(1)} %bitcast.132, f32[1,3072]{1,0:T(1,128)S(1)} %get-tuple-element.78.scale_ref), custom_call_target="tpu_custom_call" | custom-call | flops 14495514624 | bytes 37748736 | tf_op jit(solution)/shard_map/pallas_call | solution.py:146
  241.7 1.8 fusion.16
  243.5 2.5 stack.117
  246.0 3.3 copy.58
  249.3 2.8 maximum_bitcast_fusion.2
  252.1 1.7 bitcast_add_fusion.1
  255.2 1.7 select_bitcast_fusion.5
  257.5 14.9 %collective-permute-done.7 = f32[64,3072]{1,0:T(8,128)S(1)} collective-permute-done((f32[64,3072]{1,0:T(8,128)S(1)}, f32[64,3072]{1,0:T(8,128)S(1)}, u32[]{:S(2)}, u32[]{:S(2)}) %collective-permute-start.7) | collective-permute-done | bytes 786464 | tf_op jit(solution)/shard_map/ppermute | solution.py:165
  273.7 3.1 fusion.27
  278.7 22.7 %shard_map.62 = f32[256,3072]{1,0:T(8,128)S(1)} custom-call(f32[3072,3072]{1,0:T(8,128)} %a_ref.7, f32[3072,256]{1,0:T(8,128)S(1)} %bitcast.137, f32[1,3072]{1,0:T(1,128)S(1)} %get-tuple-element.78.scale_ref), custom_call_target="tpu_custom_call" | custom-call | flops 14495514624 | bytes 37748736 | tf_op jit(solution)/shard_map/pallas_call | solution.py:146
  302.9 1.8 collective-permute-start.10
  304.7 3.4 fusion.4
  312.9 1.8 fusion.17
  314.7 2.4 stack.118
  317.2 2.4 copy.59
  319.6 3.6 maximum_bitcast_fusion
  323.2 4.3 stack_reshape.6
  327.5 1.7 bitcast_add_fusion
  330.5 1.7 select_bitcast_fusion.3
  332.9 14.4 %collective-permute-done.11 = f32[64,3072]{1,0:T(8,128)S(1)} collective-permute-done((f32[64,3072]{1,0:T(8,128)S(1)}, f32[64,3072]{1,0:T(8,128)S(1)}, u32[]{:S(2)}, u32[]{:S(2)}) %collective-permute-start.11) | collective-permute-done | bytes 786464 | tf_op jit(solution)/shard_map/ppermute | solution.py:165
  350.3 14.2 %collective-permute-done.14 = f32[64,3072]{1,0:T(8,128)S(1)} collective-permute-done((f32[64,3072]{1,0:T(8,128)S(1)}, f32[64,3072]{1,0:T(8,128)S(1)}, u32[]{:S(2)}, u32[]{:S(2)}) %collective-permute-start.14) | collective-permute-done | bytes 786464 | tf_op jit(solution)/shard_map/ppermute | solution.py:165
  366.3 2.9 collective-permute-start.15
  372.6 2.1 copy.62
  376.5 2.6 copy.64
  379.1 2.1 select_bitcast_fusion.1
  389.3 2.3 maximum_bitcast_fusion.1
  391.6 3.0 stack_reshape.7
  394.6 2.7 pad_maximum_fusion.9.u_ref
  397.3 44.9 %shard_map.63 = f32[2,512,128]{2,1,0:T(8,128)} custom-call(f32[2,512,512]{2,1,0:T(8,128)} %pad_maximum_fusion.9.u_ref, f32[2,512,128]{2,1,0:T(8,128)} %jj_ref.1), custom_call_target="tpu_custom_call" | custom-call | tf_op jit(solution)/shard_map/pallas_call | solution.py:109
  442.3 1.9 copy.78
  (179 shorter events, 62.0 us)
Async XLA Ops:
  7.2 72.4 %all-gather.11.cloned.1.call-start = ((), (), s32[]{:S(2)}) async-start(), calls=%async_computation.1 | async-start | bytes 3932160 | tf_op jit(solution)/shard_map/all_gather | solution.py:221
  16.1 1.6 copy-start.41
  16.2 127.1 %all-gather.9.cloned.1.call-start = ((), (), s32[]{:S(2)}) async-start(), calls=%async_computation | async-start | bytes 3932160 | tf_op jit(solution)/shard_map/all_gather | solution.py:221
  17.4 189.6 %all-gather.13.cloned.1.call-start = ((), (), s32[]{:S(2)}) async-start(), calls=%async_computation.2 | async-start | bytes 3932160 | tf_op jit(solution)/shard_map/all_gather | solution.py:221
  79.5 1.9 copy-start.2
  105.6 4.0 collective-permute-start
  108.6 165.1 %all-gather.15.cloned.1.call-start = ((), (), s32[]{:S(2)}) async-start(), calls=%async_computation.3 | async-start | bytes 3932160 | tf_op jit(solution)/shard_map/all_gather | solution.py:221
  112.5 18.9 %collective-permute-start.1 = (f32[64,3072]{1,0:T(8,128)S(1)}, f32[64,3072]{1,0:T(8,128)S(1)}, u32[]{:S(2)}, u32[]{:S(2)}) collective-permute-start(f32[64,3072]{1,0:T(8,128)S(1)} %dynamic-slice_bitcast_fusion.7), channel_id=1, source_target_pairs={{0,2},{1,3},{2,0},{3,1},{4,6},{5,7},{6,4},{7,5},{8,10},{9,11},{10,... | collective-permute-start | bytes 2359304 | tf_op jit(solution)/shard_map/ppermute | solution.py:165
  133.5 38.8 %collective-permute-start.4 = (f32[64,3072]{1,0:T(8,128)}, f32[64,3072]{1,0:T(8,128)}, u32[]{:S(2)}, u32[]{:S(2)}) collective-permute-start(f32[64,3072]{1,0:T(8,128)} %bitcast_add_fusion.7), channel_id=1, source_target_pairs={{0,2},{1,3},{2,0},{3,1},{4,6},{5,7},{6,4},{7,5},{8,10},{9,11},{10,... | collective-permute-start | bytes 2359304 | tf_op jit(solution)/shard_map/ppermute | solution.py:165
  143.3 1.9 copy-start.4
  169.4 4.7 %collective-permute-start.2 = (f32[2,64,3072]{2,1,0:T(8,128)}, f32[2,64,3072]{2,1,0:T(8,128)}, u32[]{:S(2)}, u32[]{:S(2)}) collective-permute-start(f32[2,64,3072]{2,1,0:T(8,128)} %dynamic-slice_bitcast_fusion.2), channel_id=1, source_target_pairs={{0,1},{1,0},{2,3},{3,2},{4,5},{5,4},{6,7},{7,6},{8,9},{9,8},{10,11... | collective-permute-start | bytes 4718600 | tf_op jit(solution)/shard_map/ppermute | solution.py:165
  174.0 22.0 %collective-permute-start.5 = (f32[2,64,3072]{2,1,0:T(8,128)S(1)}, f32[2,64,3072]{2,1,0:T(8,128)S(1)}, u32[]{:S(2)}, u32[]{:S(2)}) collective-permute-start(f32[2,64,3072]{2,1,0:T(8,128)S(1)} %pad_maximum_fusion.14), channel_id=1, source_target_pairs={{0,1},{1,0},{2,3},{3,2},{4,5},{5,4},{6,7},{7,6},{8,9},{9,8},{10,11... | collective-permute-start | bytes 4718600 | tf_op jit(solution)/shard_map/ppermute | solution.py:165
  174.1 2.4 copy-start.3
  174.1 3.3 copy-start.5
  176.0 18.8 %collective-permute-start.3 = (f32[64,3072]{1,0:T(8,128)S(1)}, f32[64,3072]{1,0:T(8,128)S(1)}, u32[]{:S(2)}, u32[]{:S(2)}) collective-permute-start(f32[64,3072]{1,0:T(8,128)S(1)} %dynamic-slice_bitcast_fusion.6), channel_id=1, source_target_pairs={{0,2},{1,3},{2,0},{3,1},{4,6},{5,7},{6,4},{7,5},{8,10},{9,11},{10,... | collective-permute-start | bytes 2359304 | tf_op jit(solution)/shard_map/ppermute | solution.py:165
  195.8 41.4 %collective-permute-start.8 = (f32[64,3072]{1,0:T(8,128)}, f32[64,3072]{1,0:T(8,128)}, u32[]{:S(2)}, u32[]{:S(2)}) collective-permute-start(f32[64,3072]{1,0:T(8,128)} %bitcast_add_fusion.6), channel_id=1, source_target_pairs={{0,2},{1,3},{2,0},{3,1},{4,6},{5,7},{6,4},{7,5},{8,10},{9,11},{10,... | collective-permute-start | bytes 2359304 | tf_op jit(solution)/shard_map/ppermute | solution.py:165
  207.0 1.9 copy-start
  208.9 25.5 %copy-start.37 = (bf16[3072,256]{1,0:T(8,128)(2,1)S(1)}, bf16[3072,256]{1,0:T(8,128)(2,1)}, u32[]{:S(2)}) copy-start(bf16[3072,256]{1,0:T(8,128)(2,1)} %get-tuple-element.47) | copy-start | bytes 4718596
  208.9 25.5 %copy-start.39 = (bf16[3072,256]{1,0:T(8,128)(2,1)S(1)}, bf16[3072,256]{1,0:T(8,128)(2,1)}, u32[]{:S(2)}) copy-start(bf16[3072,256]{1,0:T(8,128)(2,1)} %get-tuple-element.82) | copy-start | bytes 4718596
  232.5 2.5 copy-start.24
  233.8 18.3 %collective-permute-start.6 = (f32[2,64,3072]{2,1,0:T(8,128)}, f32[2,64,3072]{2,1,0:T(8,128)}, u32[]{:S(2)}, u32[]{:S(2)}) collective-permute-start(f32[2,64,3072]{2,1,0:T(8,128)} %dynamic-slice_bitcast_fusion.1), channel_id=1, source_target_pairs={{0,1},{1,0},{2,3},{3,2},{4,5},{5,4},{6,7},{7,6},{8,9},{9,8},{10,11... | collective-permute-start | bytes 4718600 | tf_op jit(solution)/shard_map/ppermute | solution.py:165
  238.7 1.7 copy-start.13
  238.7 2.5 copy-start.25
  238.7 3.0 copy-start.27
  240.4 13.9 %collective-permute-start.9 = (f32[2,64,3072]{2,1,0:T(8,128)}, f32[2,64,3072]{2,1,0:T(8,128)}, u32[]{:S(2)}, u32[]{:S(2)}) collective-permute-start(f32[2,64,3072]{2,1,0:T(8,128)} %pad_maximum_fusion.15), channel_id=1, source_target_pairs={{0,1},{1,0},{2,3},{3,2},{4,5},{5,4},{6,7},{7,6},{8,9},{9,8},{10,11... | collective-permute-start | bytes 4718600 | tf_op jit(solution)/shard_map/ppermute | solution.py:165
  253.9 18.5 %collective-permute-start.7 = (f32[64,3072]{1,0:T(8,128)S(1)}, f32[64,3072]{1,0:T(8,128)S(1)}, u32[]{:S(2)}, u32[]{:S(2)}) collective-permute-start(f32[64,3072]{1,0:T(8,128)S(1)} %dynamic-slice_bitcast_fusion.5), channel_id=1, source_target_pairs={{0,2},{1,3},{2,0},{3,1},{4,6},{5,7},{6,4},{7,5},{8,10},{9,11},{10,... | collective-permute-start | bytes 2359304 | tf_op jit(solution)/shard_map/ppermute | solution.py:165
  257.5 19.4 %copy-start.22 = (f32[2,2,64,3072]{3,2,1,0:T(8,128)}, f32[2,2,64,3072]{3,2,1,0:T(8,128)S(1)}, u32[]{:S(2)}) copy-start(f32[2,2,64,3072]{3,2,1,0:T(8,128)S(1)} %copy.55) | copy-start | bytes 9437188
  273.4 34.6 %collective-permute-start.12 = (f32[64,3072]{1,0:T(8,128)}, f32[64,3072]{1,0:T(8,128)}, u32[]{:S(2)}, u32[]{:S(2)}) collective-permute-start(f32[64,3072]{1,0:T(8,128)} %bitcast_add_fusion.5), channel_id=1, source_target_pairs={{0,2},{1,3},{2,0},{3,1},{4,6},{5,7},{6,4},{7,5},{8,10},{9,11},{10,... | collective-permute-start | bytes 2359304 | tf_op jit(solution)/shard_map/ppermute | solution.py:165
  273.7 3.1 copy-start.38
  273.7 3.2 copy-start.40
  276.9 1.9 copy-start.6
  301.5 3.2 copy-start.1
  302.9 24.6 %collective-permute-start.10 = (f32[2,64,3072]{2,1,0:T(8,128)}, f32[2,64,3072]{2,1,0:T(8,128)}, u32[]{:S(2)}, u32[]{:S(2)}) collective-permute-start(f32[2,64,3072]{2,1,0:T(8,128)} %dynamic-slice_bitcast_fusion), channel_id=1, source_target_pairs={{0,1},{1,0},{2,3},{3,2},{4,5},{5,4},{6,7},{7,6},{8,9},{9,8},{10,11... | collective-permute-start | bytes 4718600 | tf_op jit(solution)/shard_map/ppermute | solution.py:165
  308.0 4.4 copy-start.26
  308.0 4.4 copy-start.28
  309.7 1.7 copy-start.9
  309.7 3.2 copy-start.23
  311.4 19.1 %collective-permute-start.13 = (f32[2,64,3072]{2,1,0:T(8,128)}, f32[2,64,3072]{2,1,0:T(8,128)}, u32[]{:S(2)}, u32[]{:S(2)}) collective-permute-start(f32[2,64,3072]{2,1,0:T(8,128)} %pad_maximum_fusion.16), channel_id=1, source_target_pairs={{0,1},{1,0},{2,3},{3,2},{4,5},{5,4},{6,7},{7,6},{8,9},{9,8},{10,11... | collective-permute-start | bytes 4718600 | tf_op jit(solution)/shard_map/ppermute | solution.py:165
  317.2 2.4 copy-start.20
  329.2 18.0 %collective-permute-start.11 = (f32[64,3072]{1,0:T(8,128)S(1)}, f32[64,3072]{1,0:T(8,128)S(1)}, u32[]{:S(2)}, u32[]{:S(2)}) collective-permute-start(f32[64,3072]{1,0:T(8,128)S(1)} %dynamic-slice_bitcast_fusion.4), channel_id=1, source_target_pairs={{0,2},{1,3},{2,0},{3,1},{4,6},{5,7},{6,4},{7,5},{8,10},{9,11},{10,... | collective-permute-start | bytes 2359304 | tf_op jit(solution)/shard_map/ppermute | solution.py:165
  347.4 1.8 copy-start.33
  347.4 1.9 copy-start.35
  347.4 17.1 %collective-permute-start.14 = (f32[64,3072]{1,0:T(8,128)S(1)}, f32[64,3072]{1,0:T(8,128)S(1)}, u32[]{:S(2)}, u32[]{:S(2)}) collective-permute-start(f32[64,3072]{1,0:T(8,128)S(1)} %bitcast_add_fusion.4), channel_id=1, source_target_pairs={{0,2},{1,3},{2,0},{3,1},{4,6},{5,7},{6,4},{7,5},{8,10},{9,11},{10,... | collective-permute-start | bytes 2359304 | tf_op jit(solution)/shard_map/ppermute | solution.py:165
  366.3 12.8 %collective-permute-start.15 = (f32[2,64,3072]{2,1,0:T(8,128)}, f32[2,64,3072]{2,1,0:T(8,128)}, u32[]{:S(2)}, u32[]{:S(2)}) collective-permute-start(f32[2,64,3072]{2,1,0:T(8,128)} %pad_maximum_fusion.17), channel_id=1, source_target_pairs={{0,1},{1,0},{2,3},{3,2},{4,5},{5,4},{6,7},{7,6},{8,9},{9,8},{10,11... | collective-permute-start | bytes 4718600 | tf_op jit(solution)/shard_map/ppermute | solution.py:165
  369.2 1.9 copy-start.31
  381.9 1.9 copy-start.36
  384.9 1.9 copy-start.32
  391.6 3.0 copy-start.19
  (15 other events, 21.0 us)
Sparse Core Ops, SparseCore 0:
  16.3 63.1 all-gather.10
  81.1 62.1 all-gather.8
  144.8 62.1 all-gather.12
  208.5 62.0 all-gather.14
